TPU v7x, 32 devices: a whole 2x2x4 slice. The times are simulated.
32 devices in a mesh: visit: 2 (over x), patch: 16 (over z, y, core).
Axes of the slice: x: 2, y: 2, z: 4, core: 2. Of those that a mesh axis runs over, the one named last changes fastest.
Arguments:
- images: bfloat16 [2, 96, 128, 512], P('visit', 'patch'), may hold values from -12 to 12
- coefficients: float32 [2, 96, 3, 40], P('visit', 'patch'), may hold values from -2 to 2
- intersection: int32 [2, 96, 2], P('visit'), may hold values from 0 to 15, as said below
- row_offset: int32 [2, 96], P('visit'), may hold values from 0 to 7
- col_offset: int32 [2, 96], P('visit'), may hold values from 0 to 511
- shifts: float32 [2, 96, 2], P('visit'), may hold values from 0 to 1
- inv_var: float32 [2, 96], P('visit'), may hold values from 0.3 to 3
Outputs:
- coadd: float32 [128, 8192], P('visit', 'patch')
- detection: float32 [128, 8192], P('visit', 'patch')
Inputs may be any that keep to these rules, and one draw needn't show every extreme that they name: intersection[v, c, 1] = intersection[v, c, 0] + 1. Within each aligned block of 6 exposures of a visit (c from b * 6 to (b + 1) * 6 - 1), no patch is named twice.
All inputs are finite; a program needn't handle non-finite values.
Results may differ from a plain program's by a relative error of at most 0.0061.
Values may be sent and summed in bfloat16 or wider, within the bound.
No kernel may reach another device: no remote copies, remote signals or barrier semaphores. Data moves between devices by JAX's collectives and lax.ppermute only.
A program may use at most 128 MiB of HBM per device.

v0:
```python
import jax
import jax.numpy as jnp
from jax import lax
from jax.sharding import PartitionSpec as P

KRAD = 10
DRAD = 4


WIDTHS_PX = (1.0, 1.7, 2.6, 3.6)


def extended(array, sides, width):
    for axis, dim in sides:
        peers, length = (lax.axis_size(axis), array.shape[dim])
        up = [(i, (i + 1) % peers) for i in range(peers - 1)]
        down = [(j, i) for i, j in up]
        last = lax.slice_in_dim(array, length - width, length, axis=dim)
        initial = lax.slice_in_dim(array, 0, width, axis=dim)
        before = lax.ppermute(last, axis, up)
        after = lax.ppermute(initial, axis, down)
        array = jnp.concatenate([before, array, after], axis=dim)
    return array


def kernel_value(offsets, width_px, degree):
    scaled = offsets / width_px
    return scaled**degree * jnp.exp(-offsets * offsets / (2.0 * width_px * width_px))


def band_tables(radius, extent):
    offsets = jnp.arange(-radius, radius + 1).astype(jnp.float32)
    distance = (jnp.arange(extent)[None, :] - jnp.arange(extent)[:, None]).astype(jnp.float32)
    inside = jnp.abs(distance) <= radius
    tables = []
    for group in range(4):
        for degree in range(4):
            profile = kernel_value(offsets, WIDTHS_PX[group], degree)
            norm_value = jnp.sqrt(jnp.sum(profile * profile))
            values = kernel_value(distance, WIDTHS_PX[group], degree) / norm_value
            tables.append(jnp.where(inside, values, 0.0).astype(jnp.bfloat16))
    return jnp.stack(tables).reshape(4, 4, extent, extent)


def match_exposure(exposure, weights, row_band, col_band, row_pos, col_pos):
    smoothed = jnp.einsum(
        "gdri,iw->gdrw", row_band, exposure, preferred_element_type=jnp.float32
    ).astype(jnp.bfloat16)
    matched = jnp.zeros(exposure.shape, jnp.float32)
    term = 0
    for group in range(4):
        for x_degree in range(4):
            count = 4 - x_degree
            response = jnp.einsum(
                "drw,xw->drx",
                smoothed[group, :count],
                col_band[group, x_degree],
                preferred_element_type=jnp.float32,
            )
            picked = weights[:, term : term + count]
            steady = jnp.sum(picked[0][:, None, None] * response, 0)
            along_rows = jnp.sum(picked[1][:, None, None] * response, 0)
            along_cols = jnp.sum(picked[2][:, None, None] * response, 0)
            matched = (
                matched + steady + row_pos[:, None] * along_rows + col_pos[None, :] * along_cols
            )
            term += count
    return matched.astype(jnp.bfloat16)


def warp_exposure(exposure, row_shift, col_shift, frac_row, frac_col, weight):
    row_count, col_count = exposure.shape
    nothing = jnp.zeros((), jnp.bfloat16)
    upper = (1.0 - frac_row).astype(jnp.bfloat16)
    lower = frac_row.astype(jnp.bfloat16)
    left = (1.0 - frac_col).astype(jnp.bfloat16)
    right = frac_col.astype(jnp.bfloat16)
    target_row = jnp.arange(row_count)[:, None]
    source_row = jnp.arange(row_count)[None, :]
    row_map = jnp.where(source_row == target_row - row_shift, upper, nothing) + jnp.where(
        source_row == target_row - row_shift - 1, lower, nothing
    )
    source_col = jnp.arange(col_count)[:, None]
    target_col = jnp.arange(col_count)[None, :]
    col_map = jnp.where(source_col == target_col - col_shift, left, nothing) + jnp.where(
        source_col == target_col - col_shift - 1, right, nothing
    )
    middle = jnp.dot(row_map, exposure, preferred_element_type=jnp.float32).astype(jnp.bfloat16)
    warped = jnp.dot(middle, col_map, preferred_element_type=jnp.float32)
    row_cover = jnp.sum(row_map.astype(jnp.float32), 1)
    col_cover = jnp.sum(col_map.astype(jnp.float32), 0)
    return (weight * warped, weight * row_cover[:, None] * col_cover[None, :])


def detect(framed, radius):
    offsets = jnp.arange(-radius, radius + 1).astype(jnp.float32)
    profile = jnp.exp(-offsets * offsets / 8.0)
    profile = profile / jnp.sqrt(jnp.sum(profile * profile))
    row_count = framed.shape[0] - 2 * radius
    col_count = framed.shape[1] - 2 * radius
    across = jnp.zeros((row_count, framed.shape[1]), jnp.float32)
    for tap_idx in range(2 * radius + 1):
        across = across + profile[tap_idx] * framed[tap_idx : tap_idx + row_count]
    result = jnp.zeros((row_count, col_count), jnp.float32)
    for tap_idx in range(2 * radius + 1):
        result = result + profile[tap_idx] * across[:, tap_idx : tap_idx + col_count]
    return result


def local(images, coefficients, intersection, row_offset, col_offset, shifts, inv_var):
    exposures = images[0]
    weights_all = coefficients[0]
    row_count = exposures.shape[1]
    col_count = exposures.shape[2]
    table = intersection[0]
    row_shifts = row_offset[0]
    col_shifts = col_offset[0]
    fractions = shifts[0]
    inverse = inv_var[0]
    own_patch = lax.axis_index("patch")
    row_band = band_tables(KRAD, row_count)
    col_band = band_tables(KRAD, col_count)
    row_pos = (2.0 * jnp.arange(row_count).astype(jnp.float32) + 1.0) / row_count - 1.0
    col_pos = (2.0 * jnp.arange(col_count).astype(jnp.float32) + 1.0) / col_count - 1.0
    matched = lax.map(
        lambda operands: match_exposure(
            operands[0], operands[1], row_band, col_band, row_pos, col_pos
        ),
        (exposures, weights_all),
    )
    empty = (
        jnp.zeros((row_count, col_count), jnp.float32),
        jnp.zeros((row_count, col_count), jnp.float32),
    )

    def add_exposure(totals, exposure, ccd, hit_first):
        col_shift = jnp.where(hit_first, col_shifts[ccd], col_shifts[ccd] - col_count)
        flux_part, cover_part = warp_exposure(
            exposure, row_shifts[ccd], col_shift, fractions[ccd, 0], fractions[ccd, 1], inverse[ccd]
        )
        return (totals[0] + flux_part, totals[1] + cover_part)

    arrived = lax.all_gather(matched, "patch", axis=0, tiled=True)

    def visit_one(offset, inner):
        hit_first = table[offset, 0] == own_patch
        hit_second = table[offset, 1] == own_patch
        exposure = lax.dynamic_index_in_dim(arrived, offset, 0, keepdims=False)
        return lax.cond(
            hit_first | hit_second,
            lambda: add_exposure(inner, exposure, offset, hit_first),
            lambda: inner,
        )

    flux_sum, cover_sum = lax.fori_loop(0, arrived.shape[0], visit_one, empty)
    flux_part, cover_part = (
        lax.psum_scatter(flux_sum, "visit", scatter_dimension=0, tiled=True),
        lax.psum_scatter(cover_sum, "visit", scatter_dimension=0, tiled=True),
    )
    coadd = flux_part / jnp.maximum(cover_part, 1.0)
    framed = extended(coadd, (("visit", 0), ("patch", 1)), DRAD)
    detection = detect(framed, DRAD)
    return (coadd, detection)


def solution(mesh):
    return jax.shard_map(
        local,
        mesh=mesh,
        in_specs=(
            P("visit", "patch", None, None),
            P("visit", "patch", None, None),
            P("visit", None, None),
            P("visit", None),
            P("visit", None),
            P("visit", None, None),
            P("visit", None),
        ),
        out_specs=(P("visit", "patch"), P("visit", "patch")),
        check_vma=False,
    )
```

profile of v0, /device:TPU:0, one launch (start us, length us, event | category | flops | bytes accessed | tf_op | source)
XLA Modules:
  0.0 678.3 jit_solution(11030103022260496552)
XLA Ops:
  32.3 1.4 fusion.115
  38.0 1.4 fusion.112
  43.7 1.4 fusion.113
  49.4 1.4 fusion.114
  51.3 119.2 %while.28 = (s32[]{:T(128)}, bf16[6,128,512]{2,1,0:T(8,128)(2,1)S(1)}, f32[6,3,40]{2,1,0:T(4,128)S(1)}, bf16[6,128,512]{1,2,0:T(8,128)(2,1)S(1)}, bf16[4,4,128,1...) while((s32[]{:T(128)}, ...), condition=%wide.region_53.54_spmd.clone.clone, body=%wide.region_16.53_spmd.clone.clone.sunk | while | flops 2971667456 | bytes 70542368 | solution.py:125
  52.3 2.0 multiply_reduce_fusion.58
  54.4 1.7 multiply_reduce_fusion.59
  62.8 8.5 %fusion.219 = bf16[6,128,512]{2,1,0:T(8,128)(2,1)S(1)} fusion(bf16[6,128,512]{2,1,0:T(8,128)(2,1)S(1)} %get-tuple-element.857, s32[]{:T(128)} %get-tuple-element.856, bf16[4,4,512,512]{3,2,1,0:T(8,128)(2,1)S(1)} %copy-done, f32[128,512]{1,0:T(8,128)S(1)} %get-tuple-element.764, f32[128,512]{1,0:T(8,128)S(1)} %get-tuple-element.765, ...), kind=kOutput, calls=%fused_computation.133.clone.1 | convolution fusion | flops 73138176 | bytes 11012660 | tf_op jit(solution)/shard_map/while/body/eval_jaxpr/drw,xw->drx/dot_general | solution.py:54
  72.2 2.0 multiply_reduce_fusion.58
  74.2 1.7 multiply_reduce_fusion.59
  82.6 8.5 %fusion.219 = bf16[6,128,512]{2,1,0:T(8,128)(2,1)S(1)} fusion(bf16[6,128,512]{2,1,0:T(8,128)(2,1)S(1)} %get-tuple-element.857, s32[]{:T(128)} %get-tuple-element.856, bf16[4,4,512,512]{3,2,1,0:T(8,128)(2,1)S(1)} %copy-done, f32[128,512]{1,0:T(8,128)S(1)} %get-tuple-element.764, f32[128,512]{1,0:T(8,128)S(1)} %get-tuple-element.765, ...), kind=kOutput, calls=%fused_computation.133.clone.1 | convolution fusion | flops 73138176 | bytes 11012660 | tf_op jit(solution)/shard_map/while/body/eval_jaxpr/drw,xw->drx/dot_general | solution.py:54
  92.0 2.0 multiply_reduce_fusion.58
  94.1 1.7 multiply_reduce_fusion.59
  102.4 8.5 %fusion.219 = bf16[6,128,512]{2,1,0:T(8,128)(2,1)S(1)} fusion(bf16[6,128,512]{2,1,0:T(8,128)(2,1)S(1)} %get-tuple-element.857, s32[]{:T(128)} %get-tuple-element.856, bf16[4,4,512,512]{3,2,1,0:T(8,128)(2,1)S(1)} %copy-done, f32[128,512]{1,0:T(8,128)S(1)} %get-tuple-element.764, f32[128,512]{1,0:T(8,128)S(1)} %get-tuple-element.765, ...), kind=kOutput, calls=%fused_computation.133.clone.1 | convolution fusion | flops 73138176 | bytes 11012660 | tf_op jit(solution)/shard_map/while/body/eval_jaxpr/drw,xw->drx/dot_general | solution.py:54
  111.8 2.0 multiply_reduce_fusion.58
  113.9 1.7 multiply_reduce_fusion.59
  122.3 8.5 %fusion.219 = bf16[6,128,512]{2,1,0:T(8,128)(2,1)S(1)} fusion(bf16[6,128,512]{2,1,0:T(8,128)(2,1)S(1)} %get-tuple-element.857, s32[]{:T(128)} %get-tuple-element.856, bf16[4,4,512,512]{3,2,1,0:T(8,128)(2,1)S(1)} %copy-done, f32[128,512]{1,0:T(8,128)S(1)} %get-tuple-element.764, f32[128,512]{1,0:T(8,128)S(1)} %get-tuple-element.765, ...), kind=kOutput, calls=%fused_computation.133.clone.1 | convolution fusion | flops 73138176 | bytes 11012660 | tf_op jit(solution)/shard_map/while/body/eval_jaxpr/drw,xw->drx/dot_general | solution.py:54
  131.7 2.0 multiply_reduce_fusion.58
  133.7 1.7 multiply_reduce_fusion.59
  142.1 8.5 %fusion.219 = bf16[6,128,512]{2,1,0:T(8,128)(2,1)S(1)} fusion(bf16[6,128,512]{2,1,0:T(8,128)(2,1)S(1)} %get-tuple-element.857, s32[]{:T(128)} %get-tuple-element.856, bf16[4,4,512,512]{3,2,1,0:T(8,128)(2,1)S(1)} %copy-done, f32[128,512]{1,0:T(8,128)S(1)} %get-tuple-element.764, f32[128,512]{1,0:T(8,128)S(1)} %get-tuple-element.765, ...), kind=kOutput, calls=%fused_computation.133.clone.1 | convolution fusion | flops 73138176 | bytes 11012660 | tf_op jit(solution)/shard_map/while/body/eval_jaxpr/drw,xw->drx/dot_general | solution.py:54
  151.5 2.0 multiply_reduce_fusion.58
  153.6 1.7 multiply_reduce_fusion.59
  161.9 8.5 %fusion.219 = bf16[6,128,512]{2,1,0:T(8,128)(2,1)S(1)} fusion(bf16[6,128,512]{2,1,0:T(8,128)(2,1)S(1)} %get-tuple-element.857, s32[]{:T(128)} %get-tuple-element.856, bf16[4,4,512,512]{3,2,1,0:T(8,128)(2,1)S(1)} %copy-done, f32[128,512]{1,0:T(8,128)S(1)} %get-tuple-element.764, f32[128,512]{1,0:T(8,128)S(1)} %get-tuple-element.765, ...), kind=kOutput, calls=%fused_computation.133.clone.1 | convolution fusion | flops 73138176 | bytes 11012660 | tf_op jit(solution)/shard_map/while/body/eval_jaxpr/drw,xw->drx/dot_general | solution.py:54
  171.5 103.3 %all-gather.2.cloned.1.call-done = bf16[96,128,512]{2,1,0:T(8,128)(2,1)} async-done(((bf16[6,128,512]{2,1,0:T(8,128)(2,1)}), bf16[96,128,512]{2,1,0:T(8,128)(2,1)}) %all-gather.2.cloned.1.call-update) | async-done | bytes 12582928 | tf_op jit(solution)/shard_map/all_gather | solution.py:143
  274.8 268.4 %while.27 = (s32[]{:T(128)}, f32[128,512]{1,0:T(8,128)S(1)}, f32[128,512]{1,0:T(8,128)S(1)}, s32[96,2]{0,1:T(2,128)S(1)}, s32[]{:T(128)}, /*index=5*/f32[96]{0:T...) while((s32[]{:T(128)}, f32[128,512]{1,0:T(8,128)S(1)}, ...), condition=%wide.region_59.60_spmd, body=%wide.region_54.59_spmd.sunk | while | flops 88949520 | bytes 1204658 | solution.py:155
  276.8 9.6 %conditional.2 = ((f32[128,512]{1,0:T(8,128)S(1)}, f32[128,512]{1,0:T(8,128)S(1)})) conditional(s32[]{:T(128)} %convert_element_type.1283, (f32[128,512]{1,0:T(8,128)S(1)}, f32[128,512]{1,0:T(8,128)S(1)}) %tuple.161, (s32[]{:T(128)}, f32[96]{0:T(128)S(1)}, s32[96]{0:T(128)S(1)}, f32[96,2]{0,1:T(2,128)S(1)}, bf16[96,128,512]{2,1,0:T(8,128)(2,1)}, ...), branch_computations={%region_55.55_spmd, %region_56.58_spmd} | conditional | flops 88949512 | bytes 1204415 | solution.py:149
  284.5 1.9 fusion.4
  304.4 9.6 %conditional.2 = ((f32[128,512]{1,0:T(8,128)S(1)}, f32[128,512]{1,0:T(8,128)S(1)})) conditional(s32[]{:T(128)} %convert_element_type.1283, (f32[128,512]{1,0:T(8,128)S(1)}, f32[128,512]{1,0:T(8,128)S(1)}) %tuple.161, (s32[]{:T(128)}, f32[96]{0:T(128)S(1)}, s32[96]{0:T(128)S(1)}, f32[96,2]{0,1:T(2,128)S(1)}, bf16[96,128,512]{2,1,0:T(8,128)(2,1)}, ...), branch_computations={%region_55.55_spmd, %region_56.58_spmd} | conditional | flops 88949512 | bytes 1204415 | solution.py:149
  312.1 1.9 fusion.4
  332.0 9.6 %conditional.2 = ((f32[128,512]{1,0:T(8,128)S(1)}, f32[128,512]{1,0:T(8,128)S(1)})) conditional(s32[]{:T(128)} %convert_element_type.1283, (f32[128,512]{1,0:T(8,128)S(1)}, f32[128,512]{1,0:T(8,128)S(1)}) %tuple.161, (s32[]{:T(128)}, f32[96]{0:T(128)S(1)}, s32[96]{0:T(128)S(1)}, f32[96,2]{0,1:T(2,128)S(1)}, bf16[96,128,512]{2,1,0:T(8,128)(2,1)}, ...), branch_computations={%region_55.55_spmd, %region_56.58_spmd} | conditional | flops 88949512 | bytes 1204415 | solution.py:149
  339.7 1.9 fusion.4
  391.4 9.6 %conditional.2 = ((f32[128,512]{1,0:T(8,128)S(1)}, f32[128,512]{1,0:T(8,128)S(1)})) conditional(s32[]{:T(128)} %convert_element_type.1283, (f32[128,512]{1,0:T(8,128)S(1)}, f32[128,512]{1,0:T(8,128)S(1)}) %tuple.161, (s32[]{:T(128)}, f32[96]{0:T(128)S(1)}, s32[96]{0:T(128)S(1)}, f32[96,2]{0,1:T(2,128)S(1)}, bf16[96,128,512]{2,1,0:T(8,128)(2,1)}, ...), branch_computations={%region_55.55_spmd, %region_56.58_spmd} | conditional | flops 88949512 | bytes 1204415 | solution.py:149
  399.1 1.9 fusion.4
  419.0 9.6 %conditional.2 = ((f32[128,512]{1,0:T(8,128)S(1)}, f32[128,512]{1,0:T(8,128)S(1)})) conditional(s32[]{:T(128)} %convert_element_type.1283, (f32[128,512]{1,0:T(8,128)S(1)}, f32[128,512]{1,0:T(8,128)S(1)}) %tuple.161, (s32[]{:T(128)}, f32[96]{0:T(128)S(1)}, s32[96]{0:T(128)S(1)}, f32[96,2]{0,1:T(2,128)S(1)}, bf16[96,128,512]{2,1,0:T(8,128)(2,1)}, ...), branch_computations={%region_55.55_spmd, %region_56.58_spmd} | conditional | flops 88949512 | bytes 1204415 | solution.py:149
  426.7 1.9 fusion.4
  438.6 9.6 %conditional.2 = ((f32[128,512]{1,0:T(8,128)S(1)}, f32[128,512]{1,0:T(8,128)S(1)})) conditional(s32[]{:T(128)} %convert_element_type.1283, (f32[128,512]{1,0:T(8,128)S(1)}, f32[128,512]{1,0:T(8,128)S(1)}) %tuple.161, (s32[]{:T(128)}, f32[96]{0:T(128)S(1)}, s32[96]{0:T(128)S(1)}, f32[96,2]{0,1:T(2,128)S(1)}, bf16[96,128,512]{2,1,0:T(8,128)(2,1)}, ...), branch_computations={%region_55.55_spmd, %region_56.58_spmd} | conditional | flops 88949512 | bytes 1204415 | solution.py:149
  446.3 1.9 fusion.4
  462.2 9.6 %conditional.2 = ((f32[128,512]{1,0:T(8,128)S(1)}, f32[128,512]{1,0:T(8,128)S(1)})) conditional(s32[]{:T(128)} %convert_element_type.1283, (f32[128,512]{1,0:T(8,128)S(1)}, f32[128,512]{1,0:T(8,128)S(1)}) %tuple.161, (s32[]{:T(128)}, f32[96]{0:T(128)S(1)}, s32[96]{0:T(128)S(1)}, f32[96,2]{0,1:T(2,128)S(1)}, bf16[96,128,512]{2,1,0:T(8,128)(2,1)}, ...), branch_computations={%region_55.55_spmd, %region_56.58_spmd} | conditional | flops 88949512 | bytes 1204415 | solution.py:149
  469.9 1.9 fusion.4
  533.6 9.6 %conditional.2 = ((f32[128,512]{1,0:T(8,128)S(1)}, f32[128,512]{1,0:T(8,128)S(1)})) conditional(s32[]{:T(128)} %convert_element_type.1283, (f32[128,512]{1,0:T(8,128)S(1)}, f32[128,512]{1,0:T(8,128)S(1)}) %tuple.161, (s32[]{:T(128)}, f32[96]{0:T(128)S(1)}, s32[96]{0:T(128)S(1)}, f32[96,2]{0,1:T(2,128)S(1)}, bf16[96,128,512]{2,1,0:T(8,128)(2,1)}, ...), branch_computations={%region_55.55_spmd, %region_56.58_spmd} | conditional | flops 88949512 | bytes 1204415 | solution.py:149
  541.3 1.9 fusion.4
  546.0 84.1 %reduce-scatter.3.cloned.1.call-done = f32[64,512]{1,0:T(8,128)} async-done(((f32[128,512]{1,0:T(8,128)}), f32[64,512]{1,0:T(8,128)}) %reduce-scatter.3.cloned.1.call-update) | async-done | bytes 131088 | tf_op jit(solution)/shard_map/reduce_scatter | solution.py:157
  630.1 14.0 %reduce-scatter.5.cloned.1.call-done = f32[64,512]{1,0:T(8,128)} async-done(((f32[128,512]{1,0:T(8,128)}), f32[64,512]{1,0:T(8,128)}) %reduce-scatter.5.cloned.1.call-update) | async-done | bytes 131088 | tf_op jit(solution)/shard_map/reduce_scatter | solution.py:158
  645.2 2.3 collective-permute-start
  648.8 4.2 collective-permute-done.1
  656.4 3.0 collective-permute-done.3
  659.6 5.7 fusion.128
  665.3 6.5 fusion.136
  (491 shorter events, 176.7 us)
Async XLA Ops:
  7.2 43.7 %copy-start.4 = (bf16[1,6,128,512]{3,2,1,0:T(8,128)(2,1)S(1)}, bf16[1,6,128,512]{3,2,1,0:T(8,128)(2,1)}, u32[]{:S(2)}) copy-start(bf16[1,6,128,512]{3,2,1,0:T(8,128)(2,1)} %param.13) | copy-start | bytes 2359300
  7.2 44.1 %copy-start.8 = (f32[1,6,3,40]{3,0,2,1:T(1,128)S(1)}, f32[1,6,3,40]{3,0,2,1:T(1,128)}, u32[]{:S(2)}) copy-start(f32[1,6,3,40]{3,0,2,1:T(1,128)} %param.14) | copy-start | bytes 8644
  7.2 267.6 %all-gather.2.cloned.1.call-start = ((), (), s32[]{:S(2)}) async-start(), calls=%async_computation.2 | async-start | bytes 13369344 | tf_op jit(solution)/shard_map/all_gather | solution.py:143
  51.3 223.5 %copy-start.6 = (s32[1,96,2]{1,2,0:T(2,128)S(1)}, s32[1,96,2]{1,2,0:T(2,128)}, u32[]{:S(2)}) copy-start(s32[1,96,2]{1,2,0:T(2,128)} %param.15) | copy-start | bytes 2308
  51.3 223.5 %copy-start.7 = (f32[1,96,2]{1,2,0:T(2,128)S(1)}, f32[1,96,2]{1,2,0:T(2,128)}, u32[]{:S(2)}) copy-start(f32[1,96,2]{1,2,0:T(2,128)} %param.18) | copy-start | bytes 2308
  51.3 223.5 %copy-start.9 = (f32[1,96]{1,0:T(1,128)S(1)}, f32[1,96]{1,0:T(1,128)}, u32[]{:S(2)}) copy-start(f32[1,96]{1,0:T(1,128)} %param.19) | copy-start | bytes 1156
  51.3 223.5 %copy-start.10 = (s32[1,96]{1,0:T(1,128)S(1)}, s32[1,96]{1,0:T(1,128)}, u32[]{:S(2)}) copy-start(s32[1,96]{1,0:T(1,128)} %param.16) | copy-start | bytes 1156
  51.3 223.5 %copy-start.11 = (s32[1,96]{1,0:T(1,128)S(1)}, s32[1,96]{1,0:T(1,128)}, u32[]{:S(2)}) copy-start(s32[1,96]{1,0:T(1,128)} %param.17) | copy-start | bytes 1156
  51.5 4.7 copy-start
  71.3 4.7 copy-start
  91.2 4.7 copy-start
  111.0 4.7 copy-start
  130.8 4.7 copy-start
  150.7 4.7 copy-start
  170.5 0.9 copy-start.5
  171.4 458.7 %reduce-scatter.3.cloned.1.call-start = ((), (), s32[]{:S(2)}) async-start(), calls=%async_computation.3 | async-start | bytes 393216 | tf_op jit(solution)/shard_map/reduce_scatter | solution.py:157
  543.3 0.7 copy-start.3
  543.3 0.8 copy-start.1
  544.0 100.2 %reduce-scatter.5.cloned.1.call-start = ((), (), s32[]{:S(2)}) async-start(), calls=%async_computation.4 | async-start | bytes 393216 | tf_op jit(solution)/shard_map/reduce_scatter | solution.py:158
  645.2 26.6 %copy-start.2 = (f32[64,512]{1,0:T(8,128)}, f32[64,512]{1,0:T(8,128)S(1)}, u32[]{:S(2)}) copy-start(f32[64,512]{1,0:T(8,128)S(1)} %maximum_divide_fusion) | copy-start | bytes 393220
  645.2 3.6 collective-permute-start
  647.5 5.5 collective-permute-start.1
  653.1 3.3 collective-permute-start.2
  654.4 5.0 collective-permute-start.3
Sparse Core Ops, SparseCore 0:
  171.6 103.1 all-gather.1
  544.1 86.0 reduce-scatter.2
  632.4 11.7 reduce-scatter.4
where the time goes:
time: 685 us; the launch traced here: 678 us
  waiting for transfers between devices  209 us (31%)
  loops' own time  159 us (23%)
  matrix products  128 us (19%)
  local copies, waits for them, and re-layouts  90.3 us (13%)
  other arithmetic  60.2 us (9%)
  between operations  25.4 us (4%)
    another operation x1, loops' own time, local(): flux_sum, cover_sum = lax.fori_loop(0, arrived.shape[0], visit_one, empty)  128 us
    dot_general x96, matrix products, match_exposure(): jnp.einsum('drw,xw->drx', smoothed[group, :count], col_band[group, x_degr...  108 us
    all_gather x1, waiting for transfers between devices, local(): arrived = lax.all_gather(matched, 'patch', axis=0, tiled=True)  103 us
    reduce_scatter x1, waiting for transfers between devices, local(): lax.psum_scatter(flux_sum, 'visit', scatter_dimension=0, tiled=True)  84.1 us
    dynamic_slice x96, local copies, waits for them, and re-layouts, visit_one(): hit_second = table[offset, 1] == own_patch  62.7 us
    another operation x96, loops' own time, visit_one(): lax.cond(hit_first | hit_second, lambda: add_exposure(inner, exposure, of...  30.3 us
    unnamed x30, other arithmetic  21.1 us
    dot_general x8, matrix products, warp_exposure(): warped = jnp.dot(middle, col_map, preferred_element_type=jnp.float32)  15.3 us
  transfers between devices with their start and end apart: 7, of which 5 were waited for; matrix products, arithmetic and copies ran while one was open for 0% of the time, Pallas kernels for 0%

commit v1 on v0

v1 whole, which is shorter than its diff:
```python
import functools
import jax
import jax.numpy as jnp
import numpy as np
from jax import lax
from jax.experimental import pallas as pl
from jax.experimental.pallas import tpu as pltpu
from jax.sharding import PartitionSpec as P

KRAD = 10
DRAD = 4
WIDTHS_PX = (1.0, 1.7, 2.6, 3.6)
LANE = 128
PAIRS = [(s, d) for s in range(4) for d in range(4)]
CHUNKS = ((0, 3), (3, 6))
VMEM_LIMIT = 56 * 1024 * 1024


def basis_taps():
    t = np.arange(-KRAD, KRAD + 1).astype(np.float32)
    taps = []
    for s, d in PAIRS:
        w = np.float32(WIDTHS_PX[s])
        profile = (t / w) ** d * np.exp(-t * t / (np.float32(2.0) * w * w))
        taps.append(profile / np.sqrt(np.sum(profile * profile)))
    return np.stack(taps).astype(np.float32).astype(jnp.bfloat16)


def column_table(taps):
    window = np.arange(2 * LANE)[:, None]
    column = np.arange(LANE)[None, :]
    tap = window - LANE // 2 - column
    inside = np.abs(tap) <= KRAD
    index = np.clip(tap + KRAD, 0, 2 * KRAD)
    blocks = [np.where(inside, row[index], row.dtype.type(0)) for row in taps]
    return np.concatenate(blocks, axis=1)


def row_table(taps):
    row = np.arange(16)[:, None]
    lane = np.arange(LANE)[None, :]
    tap = (lane - row + LANE // 2) % LANE - LANE // 2
    inside = np.abs(tap) <= KRAD
    index = np.clip(tap + KRAD, 0, 2 * KRAD)
    return np.stack([np.where(inside, t[index], t.dtype.type(0)).astype(np.float32) for t in taps])


def iota(shape, dim):
    return lax.broadcasted_iota(jnp.int32, shape, dim)


class Plan:
    def __init__(self, mesh, height, width):
        self.visits = mesh.shape["visit"]
        self.patches = mesh.shape["patch"]
        self.height = height
        self.width = width
        self.block = height // self.visits
        if self.visits == 2:
            self.useful = self.block + DRAD
            self.step, self.first = self.block - DRAD, 0
        else:
            self.useful = self.block + 2 * DRAD
            self.step, self.first = self.block, -DRAD
        self.rows = -(-(self.useful + 4) // 8) * 8

    def base(self, visit):
        return visit * self.step + self.first


def match_kernel(plan, first, where_ref, row_ref, shift_ref, coef_ref, image_ref, table_ref, tap_ref, *rest):
    outs, (grid_ref, left_ref) = rest[:-2], rest[-2:]
    step = pl.program_id(0)
    ccd = first + step
    visit = where_ref[0]
    index = where_ref[1] * where_ref[2] + ccd
    height, width = plan.height, plan.width
    tiles = width // LANE

    image = image_ref[0, 0]
    edge = jnp.zeros((height, LANE // 2), image.dtype)
    padded = jnp.concatenate([edge, image, edge], axis=1)
    for pair in range(8):
        table = table_ref[:, pair * 256 : (pair + 1) * 256]
        for t in range(tiles):
            out = jnp.dot(padded[:, t * LANE : (t + 2) * LANE], table, preferred_element_type=jnp.float32)
            out = out.astype(jnp.bfloat16)
            for half in range(2):
                g = pair * 2 + half
                grid_ref[g * height : (g + 1) * height, t * LANE : (t + 1) * LANE] = out[:, half * LANE : (half + 1) * LANE]

    local_row = iota((16, LANE), 0).astype(jnp.float32)
    lane = iota((16, LANE), 1)
    yn = (2.0 * local_row + 1.0) / height - 1.0
    for g, (s, i) in enumerate(PAIRS):
        term = s * 10 + (0, 4, 7, 9)[i]
        sums = []
        for q in range(3):
            total = coef_ref[0, ccd, q, term] * tap_ref[s * 4]
            for j in range(1, 4 - i):
                total = total + coef_ref[0, ccd, q, term + j] * tap_ref[s * 4 + j]
            sums.append(total)
        steady = sums[0] + yn * sums[1]
        flat = sums[2].astype(jnp.bfloat16)
        for b in range(height // 16):
            tall = (steady + (32.0 * b / height) * sums[1]).astype(jnp.bfloat16)
            wide = flat
            if b:
                tall = pltpu.roll(tall, 16 * b, 1)
                wide = pltpu.roll(wide, 16 * b, 1)
            if b == 0:
                tall = jnp.where(lane < LANE // 2, tall, jnp.zeros_like(tall))
                wide = jnp.where(lane < LANE // 2, wide, jnp.zeros_like(wide))
            if b == height // 16 - 1:
                tall = jnp.where(lane >= LANE // 2, tall, jnp.zeros_like(tall))
                wide = jnp.where(lane >= LANE // 2, wide, jnp.zeros_like(wide))
            left_ref[16 * b : 16 * b + 16, g * LANE : (g + 1) * LANE] = tall
            left_ref[height + 16 * b : height + 16 * b + 16, g * LANE : (g + 1) * LANE] = wide

    both = jnp.dot(left_ref[...], grid_ref[...], preferred_element_type=jnp.float32)
    xn = (2.0 * iota((height, width), 1).astype(jnp.float32) + 1.0) / width - 1.0
    matched = (both[:height] + xn * both[height:]).astype(jnp.bfloat16)

    shift = row_ref[0, index]
    frac = jnp.full((plan.rows, height), shift_ref[0, index, 0], jnp.float32)
    upper = (1.0 - frac).astype(jnp.bfloat16)
    lower = frac.astype(jnp.bfloat16)
    local = iota((plan.rows, height), 0)
    source = iota((plan.rows, height), 1)
    nothing = jnp.zeros_like(upper)
    for d, out_ref in enumerate(outs):
        sky = local + plan.base(visit ^ d)
        good = (local < plan.useful) & (sky >= 0) & (sky < height)
        gap = jnp.where(good, source - sky + shift, 2 * height)
        rows = jnp.where(gap == 0, upper, jnp.where(gap == -1, lower, nothing))
        warped = jnp.dot(rows, matched, preferred_element_type=jnp.float32)
        out_ref[0] = warped.astype(jnp.bfloat16)


def match(plan, chunk, where, row_offset, shifts, coefficients, images, table, taps):
    first, last = chunk
    count = last - first
    smem = pl.BlockSpec(memory_space=pltpu.SMEM)
    height, width = plan.height, plan.width
    return pl.pallas_call(
        functools.partial(match_kernel, plan, first),
        name="match",
        grid=(count,),
        in_specs=[
            smem,
            smem,
            smem,
            smem,
            pl.BlockSpec((1, 1, height, width), lambda e: (0, first + e, 0, 0)),
            pl.BlockSpec(table.shape, lambda e: (0, 0)),
            pl.BlockSpec(taps.shape, lambda e: (0, 0, 0)),
        ],
        out_specs=[pl.BlockSpec((1, plan.rows, width), lambda e: (e, 0, 0))] * plan.visits,
        out_shape=[jax.ShapeDtypeStruct((count, plan.rows, width), jnp.bfloat16)] * plan.visits,
        scratch_shapes=[
            pltpu.VMEM((16 * height, width), jnp.bfloat16),
            pltpu.VMEM((2 * height, 16 * LANE), jnp.bfloat16),
        ],
        compiler_params=pltpu.CompilerParams(vmem_limit_bytes=VMEM_LIMIT),
    )(where, row_offset, shifts, coefficients, images, table, taps)


def place_kernel(plan, sizes, where_ref, *refs):
    metas = refs[: plan.visits]
    sources = refs[plan.visits : -3]
    send_ref, keep_ref, strip_ref = refs[-3:]
    rows, width = plan.rows, plan.width
    strip_ref[...] = jnp.zeros_like(strip_ref)
    gap = iota((2 * LANE, LANE), 0) - iota((2 * LANE, LANE), 1) - LANE
    nothing = jnp.zeros((2 * LANE, LANE), jnp.bfloat16)
    blank = jnp.zeros((rows, LANE), jnp.bfloat16)
    tiles = width // LANE
    spot = 0
    for first, last in sizes:
        for d in range(plan.visits):
            meta_ref, source_ref = metas[d], sources[spot]
            spot += 1
            for k in range(last - first):
                index = where_ref[1] * where_ref[2] + first + k
                start = meta_ref[index, 0].astype(jnp.int32)
                rem = start & (LANE - 1)
                tile = (start >> 7) + 1
                left = jnp.full(nothing.shape, meta_ref[index, 2], jnp.float32).astype(jnp.bfloat16)
                right = jnp.full(nothing.shape, meta_ref[index, 3], jnp.float32).astype(jnp.bfloat16)
                table = jnp.where(gap == -rem, left, jnp.where(gap == -rem - 1, right, nothing))
                source = jnp.concatenate([blank, source_ref[k], blank], axis=1)
                weight = meta_ref[index, 6]
                for t in range(tiles + 1):
                    out = jnp.dot(source[:, t * LANE : (t + 2) * LANE], table, preferred_element_type=jnp.float32)
                    strip_ref[tile + t] = strip_ref[tile + t] + weight * out

    core = where_ref[3] & 1
    chip = where_ref[3] >> 1
    pick = iota((8, LANE), 0) - 4
    lane = iota((8, LANE), 1)
    pick_left = ((pick >= 0) & (lane == LANE - 4 + pick)).astype(jnp.bfloat16)
    pick_right = ((pick >= 0) & (lane == pick)).astype(jnp.bfloat16)

    def across(table, block):
        out = lax.dot_general(table, block.astype(jnp.bfloat16), (((1,), (1,)), ((), ())), preferred_element_type=jnp.float32)
        return jnp.pad(out, ((0, 0), (0, LANE - rows)))

    def emit(m, parity, out_ref):
        tile = (2 * (chip ^ m) + parity) * tiles + 1
        sides = (across(pick_left, strip_ref[tile - 1]), across(pick_right, strip_ref[tile + tiles]))
        for t in range(tiles):
            body = strip_ref[tile + t]
            if t < 2:
                body = jnp.concatenate([body[: rows - 8], body[rows - 8 :] + sides[t]], axis=0)
            out_ref[m, :, t * LANE : (t + 1) * LANE] = body.astype(out_ref.dtype)

    for m in range(plan.patches // 2):
        emit(m, 1 - core, send_ref)
        emit(m, core, keep_ref)


def place(plan, sizes, where, metas, sources):
    smem = pl.BlockSpec(memory_space=pltpu.SMEM)
    vmem = pl.BlockSpec(memory_space=pltpu.VMEM)
    half = plan.patches // 2
    return pl.pallas_call(
        functools.partial(place_kernel, plan, sizes),
        name="place",
        in_specs=[smem] * (1 + plan.visits) + [vmem] * len(sources),
        out_specs=[vmem, vmem],
        out_shape=[
            jax.ShapeDtypeStruct((half, plan.rows, plan.width), jnp.bfloat16),
            jax.ShapeDtypeStruct((half, plan.rows, plan.width), jnp.float32),
        ],
        scratch_shapes=[pltpu.VMEM((plan.patches * plan.width // LANE + 2, plan.rows, LANE), jnp.float32)],
        compiler_params=pltpu.CompilerParams(vmem_limit_bytes=VMEM_LIMIT),
    )(where, *metas, *sources)


def fold_kernel(keep_ref, got_ref, *outs):
    for m, out_ref in enumerate(outs):
        out_ref[...] = (keep_ref[m] + got_ref[m].astype(jnp.float32)).astype(out_ref.dtype)


def fold(plan, keep, got):
    vmem = pl.BlockSpec(memory_space=pltpu.VMEM)
    half = plan.patches // 2
    shape = (plan.rows, plan.width)
    return pl.pallas_call(
        fold_kernel,
        name="fold",
        in_specs=[vmem, vmem],
        out_specs=[vmem] * half,
        out_shape=[jax.ShapeDtypeStruct(shape, jnp.float32)] + [jax.ShapeDtypeStruct(shape, jnp.bfloat16)] * (half - 1),
    )(keep, got)


def cover_kernel(plan, where_ref, *refs):
    metas, out_ref = refs[:-1], refs[-1]
    rows, width = plan.rows, plan.width
    column = where_ref[3] * width
    base = plan.base(where_ref[0])
    total = jnp.zeros((LANE, width), jnp.float32)
    sides = jnp.zeros((LANE, LANE), jnp.float32)
    for meta_ref in metas:
        meta = meta_ref[...]
        count = meta.shape[0]
        local = iota((count, LANE), 1)
        sky = (local + base).astype(jnp.float32)
        oy = meta[:, 1:2]
        rho = jnp.where(sky >= oy, meta[:, 4:5], 0.0) + jnp.where(sky >= oy + 1.0, meta[:, 5:6], 0.0)
        rho = jnp.where((local < plan.useful) & (sky >= 0) & (sky < plan.height), meta[:, 6:7] * rho, 0.0)

        def kappa(place):
            gap = place.astype(jnp.float32) - meta[:, 0:1]
            return jnp.where((gap >= 0) & (gap < width), meta[:, 2:3], 0.0) + jnp.where(
                (gap >= 1) & (gap < width + 1), meta[:, 3:4], 0.0
            )

        spot = iota((count, LANE), 1)
        side = jnp.where(spot < 8, spot - 8, spot - 12 + width)
        known = ((spot >= 4) & (spot < 8)) | ((spot >= 12) & (spot < 16))
        edge = jnp.where(known, kappa(side + column), 0.0)
        dims = (((0,), (0,)), ((), ()))
        kinds = dict(preferred_element_type=jnp.float32, precision=lax.Precision.HIGHEST)
        total = total + lax.dot_general(rho, kappa(iota((count, width), 1) + column), dims, **kinds)
        sides = sides + lax.dot_general(edge, rho, dims, **kinds)
    tail = total[rows - 8 : rows]
    tail = jnp.concatenate([tail[:, :LANE] + sides[:8], tail[:, LANE : 2 * LANE] + sides[8:16], tail[:, 2 * LANE :]], axis=1)
    out_ref[...] = jnp.concatenate([total[: rows - 8], tail], axis=0)


def cover_of(plan, where, metas):
    vmem = pl.BlockSpec(memory_space=pltpu.VMEM)
    return pl.pallas_call(
        functools.partial(cover_kernel, plan),
        name="cover",
        in_specs=[pl.BlockSpec(memory_space=pltpu.SMEM)] + [vmem] * plan.visits,
        out_specs=vmem,
        out_shape=jax.ShapeDtypeStruct((plan.rows, plan.width), jnp.float32),
    )(where, *metas)


def finish_kernel(plan, filt, where_ref, cover_ref, own_ref, *refs):
    parts, (coadd_ref, detect_ref) = refs[:-2], refs[-2:]
    rows, width, block = plan.rows, plan.width, plan.block
    flux = own_ref[...]
    for part in parts:
        flux = flux + part[...].astype(jnp.float32)
    coadd = flux / jnp.maximum(cover_ref[...], 1.0)
    visit = where_ref[0]
    if plan.step == block:
        coadd_ref[...] = coadd[-plan.first : -plan.first + block]
    else:
        coadd_ref[...] = jnp.where(visit == 0, coadd[:block], coadd[DRAD : DRAD + block])

    local = iota((block, LANE), 1)
    tap = local + plan.base(visit) - visit * block - iota((block, LANE), 0)
    good = (local < plan.useful) & (jnp.abs(tap) <= DRAD)
    band = jnp.zeros((block, LANE), jnp.float32)
    for t in range(-DRAD, DRAD + 1):
        band = jnp.where(good & (tap == t), filt[t + DRAD], band)
    kinds = dict(preferred_element_type=jnp.float32, precision=lax.Precision.HIGHEST)
    tall = jnp.concatenate([coadd, jnp.zeros((LANE - rows, width), jnp.float32)], axis=0)
    down = jnp.dot(band, tall, **kinds)
    blank = jnp.zeros((LANE - 8, LANE), jnp.float32)
    dims = (((1,), (1,)), ((), ()))
    before = lax.dot_general(band, jnp.concatenate([blank, coadd[rows - 8 :, :LANE]], axis=0), dims, **kinds)
    after = lax.dot_general(band, jnp.concatenate([coadd[rows - 8 :, LANE : 2 * LANE], blank], axis=0), dims, **kinds)
    lane = iota((block, LANE), 1)
    before = jnp.where(lane >= LANE - DRAD, before, 0.0)
    after = pltpu.roll(after, LANE - DRAD, 1)
    after = jnp.where(lane < DRAD, after, 0.0)
    wide = jnp.concatenate([before, down, after], axis=1)
    total = filt[DRAD] * wide
    for t in range(1, DRAD + 1):
        total = total + filt[DRAD + t] * (pltpu.roll(wide, t, 1) + pltpu.roll(wide, width + 2 * LANE - t, 1))
    detect_ref[...] = total[:, LANE : LANE + width]


def finish(plan, where, cover, own, parts):
    vmem = pl.BlockSpec(memory_space=pltpu.VMEM)
    t = np.arange(-DRAD, DRAD + 1).astype(np.float32)
    filt = np.exp(-t * t / np.float32(8.0))
    filt = filt / np.sqrt(np.sum(filt * filt))
    filt = [float(value) for value in filt]
    shape = jax.ShapeDtypeStruct((plan.block, plan.width), jnp.float32)
    return pl.pallas_call(
        functools.partial(finish_kernel, plan, filt),
        name="finish",
        in_specs=[pl.BlockSpec(memory_space=pltpu.SMEM)] + [vmem] * (2 + len(parts)),
        out_specs=[vmem, vmem],
        out_shape=[shape, shape],
    )(where, cover, own, *parts)


def narrow(value):
    return lax.reduce_precision(value, 8, 7)


def local(mesh, images, coefficients, intersection, row_offset, col_offset, shifts, inv_var):
    count, height, width = images.shape[1:]
    plan = Plan(mesh, height, width)
    taps = basis_taps()
    table, rows = jnp.asarray(column_table(taps)), jnp.asarray(row_table(taps))
    visit, patch = lax.axis_index("visit"), lax.axis_index("patch")
    where = jnp.stack([visit, patch, jnp.int32(count), patch]).astype(jnp.int32)
    frac_row, frac_col = shifts[0, :, 0:1], shifts[0, :, 1:2]
    start = intersection[0, :, 0:1] * width + col_offset[0][:, None]
    meta = jnp.concatenate(
        [
            start.astype(jnp.float32),
            row_offset[0][:, None].astype(jnp.float32),
            narrow(1.0 - frac_col),
            narrow(frac_col),
            narrow(1.0 - frac_row),
            narrow(frac_row),
            inv_var[0][:, None],
            jnp.zeros_like(frac_row),
        ],
        axis=1,
    )

    def swap(value, axis, bit):
        return lax.ppermute(value, axis, [(i, i ^ bit) for i in range(mesh.shape[axis])])

    metas = [meta] + [swap(meta, "visit", d) for d in range(1, plan.visits)]
    sources = []
    chunks = [(lo, min(hi, count)) for lo, hi in CHUNKS]
    for chunk in chunks:
        slots = match(plan, chunk, where, row_offset, shifts, coefficients, images, table, rows)
        sources += [slots[0]] + [swap(slots[d], "visit", d) for d in range(1, plan.visits)]
    cover = cover_of(plan, where, metas)
    send, keep = place(plan, chunks, where, metas, sources)
    folded = fold(plan, keep, swap(send, "patch", 1))
    parts = [swap(folded[m], "patch", 2 * m) for m in range(1, plan.patches // 2)]
    return finish(plan, where, cover, folded[0], parts)


def solution(mesh):
    return jax.shard_map(
        functools.partial(local, mesh),
        mesh=mesh,
        in_specs=(
            P("visit", "patch", None, None),
            P("visit", "patch", None, None),
            P("visit", None, None),
            P("visit", None),
            P("visit", None),
            P("visit", None, None),
            P("visit", None),
        ),
        out_specs=(P("visit", "patch"), P("visit", "patch")),
        check_vma=False,
    )
```

time: 685 us -> 63.3 us (0.09)
  waiting for transfers between devices: 209 us -> 12.8 us
  loops' own time: 159 us -> 0 us
  matrix products: 128 us -> 0 us
  local copies, waits for them, and re-layouts: 90.3 us -> 5.09 us
  other arithmetic: 60.2 us -> 0.6 us
  Pallas kernels: 0 us -> 26.6 us
  between operations: 25.4 us -> 0.81 us
  starting transfers between devices: 6.25 us -> 17 us
    another operation x98 -> x0, loops' own time: 159 us -> none  [the longest x1 128 us: local(): flux_sum, cover_sum = lax.fori_loop(0, arrived.shape[0], visit_one, empty)]
    dot_general x110 -> x0, matrix products: 128 us -> none  [the longest x96 108 us: match_exposure(): jnp.einsum('drw,xw->drx', smoothed[group, :count], col_band[group, x_degr...]
    all_gather x1 -> x0, waiting for transfers between devices: 103 us -> none  [local(): arrived = lax.all_gather(matched, 'patch', axis=0, tiled=True)]
    reduce_scatter x2 -> x0, waiting for transfers between devices: 98.2 us -> none  [the longest x1 84.1 us: local(): lax.psum_scatter(flux_sum, 'visit', scatter_dimension=0, tiled=True)]
    dynamic_slice x128 -> x0, local copies, waits for them, and re-layouts: 81.9 us -> none  [the longest x96 62.7 us: visit_one(): hit_second = table[offset, 1] == own_patch]
    pallas_call x0 -> x6, Pallas kernels: none -> 26.6 us  [the longest x2 14 us: match(): pl.pallas_call(functools.partial(match_kernel, plan, first), name='match'...]
    unnamed x30 -> x0, other arithmetic: 21.1 us -> none
    reduce_sum x33 -> x0, other arithmetic: 14.4 us -> none  [the longest x16 10.3 us: band_tables(): norm_value = jnp.sqrt(jnp.sum(profile * profile))]
  transfers between devices with their start and end apart: 7 -> 11, of which waited for: 5 -> 4; matrix products, arithmetic and copies ran while one was open for 0% -> 0% of each run, Pallas kernels for 0% -> 15%
where the time goes in v1:
time: 63.3 us; the launch traced here: 62.8 us
  Pallas kernels  26.6 us (42%)
  starting transfers between devices  17 us (27%)
  waiting for transfers between devices  12.8 us (20%)
  local copies, waits for them, and re-layouts  5.09 us (8%)
  between operations  0.81 us (1%)
    ppermute x11, starting transfers between devices, swap(): lax.ppermute(value, axis, [(i, i ^ bit) for i in range(mesh.shape[axis])])  17 us
    pallas_call x2, Pallas kernels, match(): pl.pallas_call(functools.partial(match_kernel, plan, first), name='match'...  14 us
    ppermute x11, waiting for transfers between devices, swap(): lax.ppermute(value, axis, [(i, i ^ bit) for i in range(mesh.shape[axis])])  12.8 us
    pallas_call x1, Pallas kernels, place(): pl.pallas_call(functools.partial(place_kernel, plan, sizes), name='place'...  5.15 us
    unnamed x36, local copies, waits for them, and re-layouts  4.96 us
    pallas_call x1, Pallas kernels, finish(): pl.pallas_call(functools.partial(finish_kernel, plan, filt), name='finish...  2.64 us
    pallas_call x1, Pallas kernels, cover_of(): pl.pallas_call(functools.partial(cover_kernel, plan), name='cover', in_sp...  2.5 us
    pallas_call x1, Pallas kernels, fold(): pl.pallas_call(fold_kernel, name='fold', in_specs=[vmem, vmem], out_specs...  2.26 us
  transfers between devices with their start and end apart: 11, of which 4 were waited for; matrix products, arithmetic and copies ran while one was open for 0% of the time, Pallas kernels for 15%

profile of v1, /device:TPU:0, one launch (start us, length us, event | category | flops | bytes accessed | tf_op | source)
XLA Modules:
  0.0 62.8 jit_solution(10960554053891482206)
XLA Ops:
  0.6 1.4 %copy.25.shift_ref = f32[1,96,2]{2,1,0:T(8,128)} copy(f32[1,96,2]{1,2,0:T(2,128)} %param.14) | data formatting | bytes 1536 | tf_op args[5]
  2.0 1.3 %copy.26.coef_ref = f32[1,6,3,40]{3,2,1,0:T(4,128)} copy(f32[1,6,3,40]{3,0,2,1:T(1,128)} %param.10) | data formatting | bytes 5760 | tf_op args[1]
  3.3 0.6 pad_add_fusion.where_ref
  3.9 7.0 %match.2 = (bf16[3,72,512]{2,1,0:T(8,128)(2,1)}, bf16[3,72,512]{2,1,0:T(8,128)(2,1)}) custom-call(s32[4]{0:T(128)} %pad_add_fusion.where_ref, s32[1,96]{1,0:T(1,128)} %row_ref.3, f32[1,96,2]{2,1,0:T(8,128)} %copy.25.shift_ref, f32[1,6,3,40]{3,2,1,0:T(4,128)} %copy.26.coef_ref, bf16[1,6,128,512]{3,2,1,0:T(8,128)(2,1)} %image_ref.3, ...), custom_call_target="tpu_custom_call" | custom-call | tf_op jit(solution)/shard_map/match/pallas_call | solution.py:145
  10.9 0.0 copy-start.16
  10.9 0.0 copy-start.13
  10.9 0.0 copy-start.14
  11.0 3.0 %collective-permute-start.1 = (bf16[3,72,512]{2,1,0:T(8,128)(2,1)}, bf16[3,72,512]{2,1,0:T(8,128)(2,1)S(1)}, u32[]{:S(2)}, u32[]{:S(2)}) collective-permute-start(bf16[3,72,512]{2,1,0:T(8,128)(2,1)} %get-tuple-element.17), channel_id=1, source_target_pairs={{0,16},{16,0},{1,17},{17,1},{2,18},{18,2},{3,19},{19,3},{4,20},{20... | collective-permute-start | bytes 663560 | tf_op jit(solution)/shard_map/ppermute | solution.py:385
  14.0 7.0 %match.3 = (bf16[3,72,512]{2,1,0:T(8,128)(2,1)}, bf16[3,72,512]{2,1,0:T(8,128)(2,1)}) custom-call(s32[4]{0:T(128)} %pad_add_fusion.where_ref, s32[1,96]{1,0:T(1,128)} %row_ref.3, f32[1,96,2]{2,1,0:T(8,128)} %copy.25.shift_ref, f32[1,6,3,40]{3,2,1,0:T(4,128)} %copy.26.coef_ref, bf16[1,6,128,512]{3,2,1,0:T(8,128)(2,1)} %image_ref.3, ...), custom_call_target="tpu_custom_call" | custom-call | tf_op jit(solution)/shard_map/match/pallas_call | solution.py:145
  21.0 0.1 collective-permute-start.2
  21.1 0.0 copy-done.12
  21.1 0.0 copy-done.13
  21.2 0.0 copy-done.14
  21.2 0.1 copy.24.refs_0_
  21.3 2.0 %collective-permute-start = (f32[96,8]{1,0:T(8,128)S(1)}, f32[96,8]{1,0:T(8,128)S(1)}, u32[]{:S(2)}, u32[]{:S(2)}) collective-permute-start(f32[96,8]{1,0:T(8,128)S(1)} %copy.24.refs_0_), channel_id=1, source_target_pairs={{0,16},{16,0},{1,17},{17,1},{2,18},{18,2},{3,19},{19,3},{4,20},{20... | collective-permute-start | bytes 9224 | tf_op jit(solution)/shard_map/ppermute | solution.py:385
  23.3 5.8 %collective-permute-done.refs_1_ = f32[96,8]{1,0:T(8,128)S(1)} collective-permute-done((f32[96,8]{1,0:T(8,128)S(1)}, f32[96,8]{1,0:T(8,128)S(1)}, u32[]{:S(2)}, u32[]{:S(2)}) %collective-permute-start) | collective-permute-done | bytes 3104 | tf_op jit(solution)/shard_map/ppermute | solution.py:385
  29.2 0.0 collective-permute-done.1.refs_3_
  29.2 0.0 collective-permute-done.2.refs_5_
  29.2 0.6 copy-done.4
  29.8 0.1 copy-done.2
  29.9 0.1 copy-done.3
  30.0 5.2 %place.1 = (bf16[8,72,512]{2,1,0:T(8,128)(2,1)}, f32[8,72,512]{2,1,0:T(8,128)}) custom-call(s32[4]{0:T(128)} %pad_add_fusion.where_ref, f32[96,8]{1,0:T(8,128)} %copy-done.1, f32[96,8]{1,0:T(8,128)} %copy-done.4, bf16[3,72,512]{2,1,0:T(8,128)(2,1)} %get-tuple-element.16.refs_2_, bf16[3,72,512]{2,1,0:T(8,128)(2,1)} %copy-done.2, ...), custom_call_target="tpu_custom_call" | custom-call | tf_op jit(solution)/shard_map/place/pallas_call | solution.py:226
  35.1 0.0 collective-permute-start.3
  35.1 2.2 %collective-permute-done.3.got_ref = bf16[8,72,512]{2,1,0:T(8,128)(2,1)S(1)} collective-permute-done((bf16[8,72,512]{2,1,0:T(8,128)(2,1)}, bf16[8,72,512]{2,1,0:T(8,128)(2,1)S(1)}, u32[]{:S(2)}, u32[]{:S(2)}) %collective-permute-start.3) | collective-permute-done | bytes 589856 | tf_op jit(solution)/shard_map/ppermute | solution.py:385
  37.3 0.8 %copy-done = bf16[8,72,512]{2,1,0:T(8,128)(2,1)} copy-done((bf16[8,72,512]{2,1,0:T(8,128)(2,1)}, bf16[8,72,512]{2,1,0:T(8,128)(2,1)S(1)}, u32[]{:S(2)}) %copy-start) | copy-done | bytes 589848
  38.2 2.3 %fold.1 = (f32[72,512]{1,0:T(8,128)}, bf16[72,512]{1,0:T(8,128)(2,1)}, bf16[72,512]{1,0:T(8,128)(2,1)}, bf16[72,512]{1,0:T(8,128)(2,1)}, bf16[72,512]{1,0:T(8,12...) custom-call(f32[8,72,512]{2,1,0:T(8,128)} %get-tuple-element.20.keep_ref, ...), custom_call_target="tpu_custom_call" | custom-call | tf_op jit(solution)/shard_map/fold/pallas_call | solution.py:249
  40.4 4.5 %collective-permute-start.10 = (bf16[72,512]{1,0:T(8,128)(2,1)}, bf16[72,512]{1,0:T(8,128)(2,1)S(1)}, u32[]{:S(2)}, u32[]{:S(2)}) collective-permute-start(bf16[72,512]{1,0:T(8,128)(2,1)} %get-tuple-element.29), channel_id=1, source_target_pairs={{0,14},{1,15},{2,12},{3,13},{4,10},{5,11},{6,8},{7,9},{8,6},{9,7},... | collective-permute-start | bytes 221192 | tf_op jit(solution)/shard_map/ppermute | solution.py:385
  45.0 0.5 collective-permute-start.4
  45.5 0.0 collective-permute-start.5
  45.5 3.0 %collective-permute-start.6 = (bf16[72,512]{1,0:T(8,128)(2,1)}, bf16[72,512]{1,0:T(8,128)(2,1)S(1)}, u32[]{:S(2)}, u32[]{:S(2)}) collective-permute-start(bf16[72,512]{1,0:T(8,128)(2,1)} %get-tuple-element.25), channel_id=1, source_target_pairs={{0,6},{1,7},{2,4},{3,5},{4,2},{5,3},{6,0},{7,1},{8,14},{9,15},{10,... | collective-permute-start | bytes 221192 | tf_op jit(solution)/shard_map/ppermute | solution.py:385
  48.5 0.0 collective-permute-start.7
  48.5 0.0 collective-permute-done.10.refs_6_
  48.5 2.9 %collective-permute-start.8 = (bf16[72,512]{1,0:T(8,128)(2,1)}, bf16[72,512]{1,0:T(8,128)(2,1)S(1)}, u32[]{:S(2)}, u32[]{:S(2)}) collective-permute-start(bf16[72,512]{1,0:T(8,128)(2,1)} %get-tuple-element.27), channel_id=1, source_target_pairs={{0,10},{1,11},{2,8},{3,9},{4,14},{5,15},{6,12},{7,13},{8,2},{9,3},... | collective-permute-start | bytes 221192 | tf_op jit(solution)/shard_map/ppermute | solution.py:385
  51.3 0.0 collective-permute-done.4.refs_0_
  51.3 0.9 %collective-permute-start.9 = (bf16[72,512]{1,0:T(8,128)(2,1)}, bf16[72,512]{1,0:T(8,128)(2,1)S(1)}, u32[]{:S(2)}, u32[]{:S(2)}) collective-permute-start(bf16[72,512]{1,0:T(8,128)(2,1)} %get-tuple-element.28), channel_id=1, source_target_pairs={{0,12},{1,13},{2,14},{3,15},{4,8},{5,9},{6,10},{7,11},{8,4},{9,5},... | collective-permute-start | bytes 221192 | tf_op jit(solution)/shard_map/ppermute | solution.py:385
  52.3 2.5 %cover.1.cover_ref = f32[72,512]{1,0:T(8,128)} custom-call(s32[4]{0:T(128)} %pad_add_fusion.where_ref, f32[96,8]{1,0:T(8,128)} %copy-done.1, f32[96,8]{1,0:T(8,128)} %copy-done.4), custom_call_target="tpu_custom_call" | custom-call | tf_op jit(solution)/shard_map/cover/pallas_call | solution.py:295
  54.8 0.0 collective-permute-done.5.refs_1_
  54.8 0.0 collective-permute-done.6.refs_2_
  54.8 2.1 %collective-permute-done.7.refs_3_ = bf16[72,512]{1,0:T(8,128)(2,1)S(1)} collective-permute-done((bf16[72,512]{1,0:T(8,128)(2,1)}, bf16[72,512]{1,0:T(8,128)(2,1)S(1)}, u32[]{:S(2)}, u32[]{:S(2)}) %collective-permute-start.7) | collective-permute-done | bytes 73760 | tf_op jit(solution)/shard_map/ppermute | solution.py:385
  56.9 2.6 %collective-permute-done.8.refs_4_ = bf16[72,512]{1,0:T(8,128)(2,1)S(1)} collective-permute-done((bf16[72,512]{1,0:T(8,128)(2,1)}, bf16[72,512]{1,0:T(8,128)(2,1)S(1)}, u32[]{:S(2)}, u32[]{:S(2)}) %collective-permute-start.8) | collective-permute-done | bytes 73760 | tf_op jit(solution)/shard_map/ppermute | solution.py:385
  59.5 0.0 collective-permute-done.9.refs_5_
  59.5 0.0 copy-done.6
  59.5 0.0 copy-done.7
  59.5 0.0 copy-done.8
  59.5 0.0 copy-done.9
  59.5 0.6 copy-done.10
  60.1 0.0 copy-done.11
  60.2 2.6 %finish.1 = (f32[64,512]{1,0:T(8,128)}, f32[64,512]{1,0:T(8,128)}) custom-call(s32[4]{0:T(128)} %pad_add_fusion.where_ref, f32[72,512]{1,0:T(8,128)} %cover.1.cover_ref, f32[72,512]{1,0:T(8,128)} %get-tuple-element.22.own_ref, bf16[72,512]{1,0:T(8,128)(2,1)} %copy-done.6, bf16[72,512]{1,0:T(8,128)(2,1)} %copy-done.7, bf16[72,512]{1,0:T(8,128)(2,1)} %copy-done.8, ...), custom_call_target="tpu_custom_call" | custom-call | tf_op jit(solution)/shard_map/finish/pallas_call | solution.py:348
  (23 shorter events, 0.1 us)
Async XLA Ops:
  10.9 10.2 %copy-start.12 = (f32[1,96,2]{1,2,0:T(2,128)S(1)}, f32[1,96,2]{1,2,0:T(2,128)}, u32[]{:S(2)}) copy-start(f32[1,96,2]{1,2,0:T(2,128)} %param.14) | copy-start | bytes 2308
  10.9 10.2 %copy-start.15 = (s32[1,96,2]{1,2,0:T(2,128)S(1)}, s32[1,96,2]{1,2,0:T(2,128)}, u32[]{:S(2)}) copy-start(s32[1,96,2]{1,2,0:T(2,128)} %param.11) | copy-start | bytes 2308
  10.9 10.2 %copy-start.16 = (s32[1,96]{1,0:T(1,128)S(1)}, s32[1,96]{1,0:T(1,128)}, u32[]{:S(2)}) copy-start(s32[1,96]{1,0:T(1,128)} %param.13) | copy-start | bytes 1156
  10.9 10.2 %copy-start.13 = (s32[1,96]{1,0:T(1,128)S(1)}, s32[1,96]{1,0:T(1,128)}, u32[]{:S(2)}) copy-start(s32[1,96]{1,0:T(1,128)} %row_ref.3) | copy-start | bytes 1156
  10.9 10.2 %copy-start.14 = (f32[1,96]{1,0:T(1,128)S(1)}, f32[1,96]{1,0:T(1,128)}, u32[]{:S(2)}) copy-start(f32[1,96]{1,0:T(1,128)} %param.15) | copy-start | bytes 1156
  11.0 18.2 %collective-permute-start.1 = (bf16[3,72,512]{2,1,0:T(8,128)(2,1)}, bf16[3,72,512]{2,1,0:T(8,128)(2,1)S(1)}, u32[]{:S(2)}, u32[]{:S(2)}) collective-permute-start(bf16[3,72,512]{2,1,0:T(8,128)(2,1)} %get-tuple-element.17), channel_id=1, source_target_pairs={{0,16},{16,0},{1,17},{17,1},{2,18},{18,2},{3,19},{19,3},{4,20},{20... | collective-permute-start | bytes 663560 | tf_op jit(solution)/shard_map/ppermute | solution.py:385
  21.0 8.2 %collective-permute-start.2 = (bf16[3,72,512]{2,1,0:T(8,128)(2,1)}, bf16[3,72,512]{2,1,0:T(8,128)(2,1)S(1)}, u32[]{:S(2)}, u32[]{:S(2)}) collective-permute-start(bf16[3,72,512]{2,1,0:T(8,128)(2,1)} %get-tuple-element.19), channel_id=1, source_target_pairs={{0,16},{16,0},{1,17},{17,1},{2,18},{18,2},{3,19},{19,3},{4,20},{20... | collective-permute-start | bytes 663560 | tf_op jit(solution)/shard_map/ppermute | solution.py:385
  21.3 7.9 %copy-start.1 = (f32[96,8]{1,0:T(8,128)}, f32[96,8]{1,0:T(8,128)S(1)}, u32[]{:S(2)}) copy-start(f32[96,8]{1,0:T(8,128)S(1)} %copy.24.refs_0_) | copy-start | bytes 9220
  21.3 7.9 %collective-permute-start = (f32[96,8]{1,0:T(8,128)S(1)}, f32[96,8]{1,0:T(8,128)S(1)}, u32[]{:S(2)}, u32[]{:S(2)}) collective-permute-start(f32[96,8]{1,0:T(8,128)S(1)} %copy.24.refs_0_), channel_id=1, source_target_pairs={{0,16},{16,0},{1,17},{17,1},{2,18},{18,2},{3,19},{19,3},{4,20},{20... | collective-permute-start | bytes 9224 | tf_op jit(solution)/shard_map/ppermute | solution.py:385
  29.2 0.6 copy-start.4
  29.2 0.7 %copy-start.2 = (bf16[3,72,512]{2,1,0:T(8,128)(2,1)}, bf16[3,72,512]{2,1,0:T(8,128)(2,1)S(1)}, u32[]{:S(2)}) copy-start(bf16[3,72,512]{2,1,0:T(8,128)(2,1)S(1)} %collective-permute-done.1.refs_3_) | copy-start | bytes 663556
  29.2 0.8 %copy-start.3 = (bf16[3,72,512]{2,1,0:T(8,128)(2,1)}, bf16[3,72,512]{2,1,0:T(8,128)(2,1)S(1)}, u32[]{:S(2)}) copy-start(bf16[3,72,512]{2,1,0:T(8,128)(2,1)S(1)} %collective-permute-done.2.refs_5_) | copy-start | bytes 663556
  35.1 2.2 %collective-permute-start.3 = (bf16[8,72,512]{2,1,0:T(8,128)(2,1)}, bf16[8,72,512]{2,1,0:T(8,128)(2,1)S(1)}, u32[]{:S(2)}, u32[]{:S(2)}) collective-permute-start(bf16[8,72,512]{2,1,0:T(8,128)(2,1)} %get-tuple-element.21), channel_id=1, source_target_pairs={{0,1},{1,0},{2,3},{3,2},{4,5},{5,4},{6,7},{7,6},{8,9},{9,8},{10,11... | collective-permute-start | bytes 1769480 | tf_op jit(solution)/shard_map/ppermute | solution.py:385
  37.3 0.8 %copy-start = (bf16[8,72,512]{2,1,0:T(8,128)(2,1)}, bf16[8,72,512]{2,1,0:T(8,128)(2,1)S(1)}, u32[]{:S(2)}) copy-start(bf16[8,72,512]{2,1,0:T(8,128)(2,1)S(1)} %collective-permute-done.3.got_ref) | copy-start | bytes 1769476
  40.4 8.0 %collective-permute-start.10 = (bf16[72,512]{1,0:T(8,128)(2,1)}, bf16[72,512]{1,0:T(8,128)(2,1)S(1)}, u32[]{:S(2)}, u32[]{:S(2)}) collective-permute-start(bf16[72,512]{1,0:T(8,128)(2,1)} %get-tuple-element.29), channel_id=1, source_target_pairs={{0,14},{1,15},{2,12},{3,13},{4,10},{5,11},{6,8},{7,9},{8,6},{9,7},... | collective-permute-start | bytes 221192 | tf_op jit(solution)/shard_map/ppermute | solution.py:385
  45.0 6.4 %collective-permute-start.4 = (bf16[72,512]{1,0:T(8,128)(2,1)}, bf16[72,512]{1,0:T(8,128)(2,1)S(1)}, u32[]{:S(2)}, u32[]{:S(2)}) collective-permute-start(bf16[72,512]{1,0:T(8,128)(2,1)} %get-tuple-element.23), channel_id=1, source_target_pairs={{0,2},{1,3},{2,0},{3,1},{4,6},{5,7},{6,4},{7,5},{8,10},{9,11},{10,... | collective-permute-start | bytes 221192 | tf_op jit(solution)/shard_map/ppermute | solution.py:385
  45.5 9.3 %collective-permute-start.5 = (bf16[72,512]{1,0:T(8,128)(2,1)}, bf16[72,512]{1,0:T(8,128)(2,1)S(1)}, u32[]{:S(2)}, u32[]{:S(2)}) collective-permute-start(bf16[72,512]{1,0:T(8,128)(2,1)} %get-tuple-element.24), channel_id=1, source_target_pairs={{0,4},{1,5},{2,6},{3,7},{4,0},{5,1},{6,2},{7,3},{8,12},{9,13},{10,... | collective-permute-start | bytes 221192 | tf_op jit(solution)/shard_map/ppermute | solution.py:385
  45.5 9.3 %collective-permute-start.6 = (bf16[72,512]{1,0:T(8,128)(2,1)}, bf16[72,512]{1,0:T(8,128)(2,1)S(1)}, u32[]{:S(2)}, u32[]{:S(2)}) collective-permute-start(bf16[72,512]{1,0:T(8,128)(2,1)} %get-tuple-element.25), channel_id=1, source_target_pairs={{0,6},{1,7},{2,4},{3,5},{4,2},{5,3},{6,0},{7,1},{8,14},{9,15},{10,... | collective-permute-start | bytes 221192 | tf_op jit(solution)/shard_map/ppermute | solution.py:385
  48.5 8.4 %collective-permute-start.7 = (bf16[72,512]{1,0:T(8,128)(2,1)}, bf16[72,512]{1,0:T(8,128)(2,1)S(1)}, u32[]{:S(2)}, u32[]{:S(2)}) collective-permute-start(bf16[72,512]{1,0:T(8,128)(2,1)} %get-tuple-element.26), channel_id=1, source_target_pairs={{0,8},{1,9},{2,10},{3,11},{4,12},{5,13},{6,14},{7,15},{8,0},{9,1},... | collective-permute-start | bytes 221192 | tf_op jit(solution)/shard_map/ppermute | solution.py:385
  48.5 11.0 %copy-start.5 = (bf16[72,512]{1,0:T(8,128)(2,1)}, bf16[72,512]{1,0:T(8,128)(2,1)S(1)}, u32[]{:S(2)}) copy-start(bf16[72,512]{1,0:T(8,128)(2,1)S(1)} %collective-permute-done.10.refs_6_) | copy-start | bytes 221188
  48.5 11.0 %collective-permute-start.8 = (bf16[72,512]{1,0:T(8,128)(2,1)}, bf16[72,512]{1,0:T(8,128)(2,1)S(1)}, u32[]{:S(2)}, u32[]{:S(2)}) collective-permute-start(bf16[72,512]{1,0:T(8,128)(2,1)} %get-tuple-element.27), channel_id=1, source_target_pairs={{0,10},{1,11},{2,8},{3,9},{4,14},{5,15},{6,12},{7,13},{8,2},{9,3},... | collective-permute-start | bytes 221192 | tf_op jit(solution)/shard_map/ppermute | solution.py:385
  51.3 8.2 %copy-start.6 = (bf16[72,512]{1,0:T(8,128)(2,1)}, bf16[72,512]{1,0:T(8,128)(2,1)S(1)}, u32[]{:S(2)}) copy-start(bf16[72,512]{1,0:T(8,128)(2,1)S(1)} %collective-permute-done.4.refs_0_) | copy-start | bytes 221188
  51.3 8.2 %collective-permute-start.9 = (bf16[72,512]{1,0:T(8,128)(2,1)}, bf16[72,512]{1,0:T(8,128)(2,1)S(1)}, u32[]{:S(2)}, u32[]{:S(2)}) collective-permute-start(bf16[72,512]{1,0:T(8,128)(2,1)} %get-tuple-element.28), channel_id=1, source_target_pairs={{0,12},{1,13},{2,14},{3,15},{4,8},{5,9},{6,10},{7,11},{8,4},{9,5},... | collective-permute-start | bytes 221192 | tf_op jit(solution)/shard_map/ppermute | solution.py:385
  54.8 4.7 %copy-start.7 = (bf16[72,512]{1,0:T(8,128)(2,1)}, bf16[72,512]{1,0:T(8,128)(2,1)S(1)}, u32[]{:S(2)}) copy-start(bf16[72,512]{1,0:T(8,128)(2,1)S(1)} %collective-permute-done.5.refs_1_) | copy-start | bytes 221188
  54.8 4.7 %copy-start.8 = (bf16[72,512]{1,0:T(8,128)(2,1)}, bf16[72,512]{1,0:T(8,128)(2,1)S(1)}, u32[]{:S(2)}) copy-start(bf16[72,512]{1,0:T(8,128)(2,1)S(1)} %collective-permute-done.6.refs_2_) | copy-start | bytes 221188
  56.9 2.7 %copy-start.9 = (bf16[72,512]{1,0:T(8,128)(2,1)}, bf16[72,512]{1,0:T(8,128)(2,1)S(1)}, u32[]{:S(2)}) copy-start(bf16[72,512]{1,0:T(8,128)(2,1)S(1)} %collective-permute-done.7.refs_3_) | copy-start | bytes 221188
  59.5 0.6 copy-start.10
  59.5 0.7 %copy-start.11 = (bf16[72,512]{1,0:T(8,128)(2,1)}, bf16[72,512]{1,0:T(8,128)(2,1)S(1)}, u32[]{:S(2)}) copy-start(bf16[72,512]{1,0:T(8,128)(2,1)S(1)} %collective-permute-done.9.refs_5_) | copy-start | bytes 221188

commit v2 on v1

--- a/solution.py
+++ b/solution.py
@@ -13,7 +13,7 @@
 LANE = 128
 PAIRS = [(s, d) for s in range(4) for d in range(4)]
 CHUNKS = ((0, 3), (3, 6))
-VMEM_LIMIT = 56 * 1024 * 1024
+MIB = 1024 * 1024
 
 
 def basis_taps():
@@ -68,12 +68,12 @@
         return visit * self.step + self.first
 
 
-def match_kernel(plan, first, where_ref, row_ref, shift_ref, coef_ref, image_ref, table_ref, tap_ref, *rest):
+def match_kernel(plan, first, total, row_ref, shift_ref, coef_ref, image_ref, table_ref, tap_ref, *rest):
     outs, (grid_ref, left_ref) = rest[:-2], rest[-2:]
     step = pl.program_id(0)
     ccd = first + step
-    visit = where_ref[0]
-    index = where_ref[1] * where_ref[2] + ccd
+    visit = lax.axis_index("visit")
+    index = lax.axis_index("patch") * total + ccd
     height, width = plan.height, plan.width
     tiles = width // LANE
 
@@ -96,9 +96,9 @@
         term = s * 10 + (0, 4, 7, 9)[i]
         sums = []
         for q in range(3):
-            total = coef_ref[0, ccd, q, term] * tap_ref[s * 4]
+            total = coef_ref[ccd, q, 0, term] * tap_ref[s * 4]
             for j in range(1, 4 - i):
-                total = total + coef_ref[0, ccd, q, term + j] * tap_ref[s * 4 + j]
+                total = total + coef_ref[ccd, q, 0, term + j] * tap_ref[s * 4 + j]
             sums.append(total)
         steady = sums[0] + yn * sums[1]
         flat = sums[2].astype(jnp.bfloat16)
@@ -122,7 +122,7 @@
     matched = (both[:height] + xn * both[height:]).astype(jnp.bfloat16)
 
     shift = row_ref[0, index]
-    frac = jnp.full((plan.rows, height), shift_ref[0, index, 0], jnp.float32)
+    frac = jnp.full((plan.rows, height), shift_ref[0, 0, index], jnp.float32)
     upper = (1.0 - frac).astype(jnp.bfloat16)
     lower = frac.astype(jnp.bfloat16)
     local = iota((plan.rows, height), 0)
@@ -137,17 +137,16 @@
         out_ref[0] = warped.astype(jnp.bfloat16)
 
 
-def match(plan, chunk, where, row_offset, shifts, coefficients, images, table, taps):
+def match(plan, chunk, row_offset, shifts, coefficients, images, table, taps):
     first, last = chunk
     count = last - first
     smem = pl.BlockSpec(memory_space=pltpu.SMEM)
     height, width = plan.height, plan.width
     return pl.pallas_call(
-        functools.partial(match_kernel, plan, first),
+        functools.partial(match_kernel, plan, first, images.shape[1]),
         name="match",
         grid=(count,),
         in_specs=[
-            smem,
             smem,
             smem,
             smem,
@@ -161,15 +160,16 @@
             pltpu.VMEM((16 * height, width), jnp.bfloat16),
             pltpu.VMEM((2 * height, 16 * LANE), jnp.bfloat16),
         ],
-        compiler_params=pltpu.CompilerParams(vmem_limit_bytes=VMEM_LIMIT),
-    )(where, row_offset, shifts, coefficients, images, table, taps)
-
-
-def place_kernel(plan, sizes, where_ref, *refs):
+        compiler_params=pltpu.CompilerParams(vmem_limit_bytes=20 * MIB),
+    )(row_offset, shifts, coefficients, images, table, taps)
+
+
+def place_kernel(plan, sizes, total, *refs):
     metas = refs[: plan.visits]
     sources = refs[plan.visits : -3]
     send_ref, keep_ref, strip_ref = refs[-3:]
     rows, width = plan.rows, plan.width
+    patch = lax.axis_index("patch")
     strip_ref[...] = jnp.zeros_like(strip_ref)
     gap = iota((2 * LANE, LANE), 0) - iota((2 * LANE, LANE), 1) - LANE
     nothing = jnp.zeros((2 * LANE, LANE), jnp.bfloat16)
@@ -181,7 +181,7 @@
             meta_ref, source_ref = metas[d], sources[spot]
             spot += 1
             for k in range(last - first):
-                index = where_ref[1] * where_ref[2] + first + k
+                index = patch * total + first + k
                 start = meta_ref[index, 0].astype(jnp.int32)
                 rem = start & (LANE - 1)
                 tile = (start >> 7) + 1
@@ -194,8 +194,8 @@
                     out = jnp.dot(source[:, t * LANE : (t + 2) * LANE], table, preferred_element_type=jnp.float32)
                     strip_ref[tile + t] = strip_ref[tile + t] + weight * out
 
-    core = where_ref[3] & 1
-    chip = where_ref[3] >> 1
+    core = patch & 1
+    chip = patch >> 1
     pick = iota((8, LANE), 0) - 4
     lane = iota((8, LANE), 1)
     pick_left = ((pick >= 0) & (lane == LANE - 4 + pick)).astype(jnp.bfloat16)
@@ -219,22 +219,22 @@
         emit(m, core, keep_ref)
 
 
-def place(plan, sizes, where, metas, sources):
+def place(plan, sizes, total, metas, sources):
     smem = pl.BlockSpec(memory_space=pltpu.SMEM)
     vmem = pl.BlockSpec(memory_space=pltpu.VMEM)
     half = plan.patches // 2
     return pl.pallas_call(
-        functools.partial(place_kernel, plan, sizes),
+        functools.partial(place_kernel, plan, sizes, total),
         name="place",
-        in_specs=[smem] * (1 + plan.visits) + [vmem] * len(sources),
+        in_specs=[smem] * plan.visits + [vmem] * len(sources),
         out_specs=[vmem, vmem],
         out_shape=[
             jax.ShapeDtypeStruct((half, plan.rows, plan.width), jnp.bfloat16),
             jax.ShapeDtypeStruct((half, plan.rows, plan.width), jnp.float32),
         ],
         scratch_shapes=[pltpu.VMEM((plan.patches * plan.width // LANE + 2, plan.rows, LANE), jnp.float32)],
-        compiler_params=pltpu.CompilerParams(vmem_limit_bytes=VMEM_LIMIT),
-    )(where, *metas, *sources)
+        compiler_params=pltpu.CompilerParams(vmem_limit_bytes=16 * MIB),
+    )(*metas, *sources)
 
 
 def fold_kernel(keep_ref, got_ref, *outs):
@@ -252,14 +252,15 @@
         in_specs=[vmem, vmem],
         out_specs=[vmem] * half,
         out_shape=[jax.ShapeDtypeStruct(shape, jnp.float32)] + [jax.ShapeDtypeStruct(shape, jnp.bfloat16)] * (half - 1),
+        compiler_params=pltpu.CompilerParams(vmem_limit_bytes=10 * MIB),
     )(keep, got)
 
 
-def cover_kernel(plan, where_ref, *refs):
+def cover_kernel(plan, *refs):
     metas, out_ref = refs[:-1], refs[-1]
     rows, width = plan.rows, plan.width
-    column = where_ref[3] * width
-    base = plan.base(where_ref[0])
+    column = lax.axis_index("patch") * width
+    base = plan.base(lax.axis_index("visit"))
     total = jnp.zeros((LANE, width), jnp.float32)
     sides = jnp.zeros((LANE, LANE), jnp.float32)
     for meta_ref in metas:
@@ -290,25 +291,26 @@
     out_ref[...] = jnp.concatenate([total[: rows - 8], tail], axis=0)
 
 
-def cover_of(plan, where, metas):
+def cover_of(plan, metas):
     vmem = pl.BlockSpec(memory_space=pltpu.VMEM)
     return pl.pallas_call(
         functools.partial(cover_kernel, plan),
         name="cover",
-        in_specs=[pl.BlockSpec(memory_space=pltpu.SMEM)] + [vmem] * plan.visits,
+        in_specs=[vmem] * plan.visits,
         out_specs=vmem,
         out_shape=jax.ShapeDtypeStruct((plan.rows, plan.width), jnp.float32),
-    )(where, *metas)
-
-
-def finish_kernel(plan, filt, where_ref, cover_ref, own_ref, *refs):
+        compiler_params=pltpu.CompilerParams(vmem_limit_bytes=10 * MIB),
+    )(*metas)
+
+
+def finish_kernel(plan, filt, cover_ref, own_ref, *refs):
     parts, (coadd_ref, detect_ref) = refs[:-2], refs[-2:]
     rows, width, block = plan.rows, plan.width, plan.block
     flux = own_ref[...]
     for part in parts:
         flux = flux + part[...].astype(jnp.float32)
     coadd = flux / jnp.maximum(cover_ref[...], 1.0)
-    visit = where_ref[0]
+    visit = lax.axis_index("visit")
     if plan.step == block:
         coadd_ref[...] = coadd[-plan.first : -plan.first + block]
     else:
@@ -338,7 +340,7 @@
     detect_ref[...] = total[:, LANE : LANE + width]
 
 
-def finish(plan, where, cover, own, parts):
+def finish(plan, cover, own, parts):
     vmem = pl.BlockSpec(memory_space=pltpu.VMEM)
     t = np.arange(-DRAD, DRAD + 1).astype(np.float32)
     filt = np.exp(-t * t / np.float32(8.0))
@@ -348,10 +350,11 @@
     return pl.pallas_call(
         functools.partial(finish_kernel, plan, filt),
         name="finish",
-        in_specs=[pl.BlockSpec(memory_space=pltpu.SMEM)] + [vmem] * (2 + len(parts)),
+        in_specs=[vmem] * (2 + len(parts)),
         out_specs=[vmem, vmem],
         out_shape=[shape, shape],
-    )(where, cover, own, *parts)
+        compiler_params=pltpu.CompilerParams(vmem_limit_bytes=10 * MIB),
+    )(cover, own, *parts)
 
 
 def narrow(value):
@@ -363,8 +366,6 @@
     plan = Plan(mesh, height, width)
     taps = basis_taps()
     table, rows = jnp.asarray(column_table(taps)), jnp.asarray(row_table(taps))
-    visit, patch = lax.axis_index("visit"), lax.axis_index("patch")
-    where = jnp.stack([visit, patch, jnp.int32(count), patch]).astype(jnp.int32)
     frac_row, frac_col = shifts[0, :, 0:1], shifts[0, :, 1:2]
     start = intersection[0, :, 0:1] * width + col_offset[0][:, None]
     meta = jnp.concatenate(
@@ -381,6 +382,8 @@
         axis=1,
     )
 
+    sides, factors = jnp.transpose(shifts, (0, 2, 1)), jnp.transpose(coefficients, (1, 2, 0, 3))
+
     def swap(value, axis, bit):
         return lax.ppermute(value, axis, [(i, i ^ bit) for i in range(mesh.shape[axis])])
 
@@ -388,13 +391,13 @@
     sources = []
     chunks = [(lo, min(hi, count)) for lo, hi in CHUNKS]
     for chunk in chunks:
-        slots = match(plan, chunk, where, row_offset, shifts, coefficients, images, table, rows)
+        slots = match(plan, chunk, row_offset, sides, factors, images, table, rows)
         sources += [slots[0]] + [swap(slots[d], "visit", d) for d in range(1, plan.visits)]
-    cover = cover_of(plan, where, metas)
-    send, keep = place(plan, chunks, where, metas, sources)
+    cover = cover_of(plan, metas)
+    send, keep = place(plan, chunks, count, metas, sources)
     folded = fold(plan, keep, swap(send, "patch", 1))
     parts = [swap(folded[m], "patch", 2 * m) for m in range(1, plan.patches // 2)]
-    return finish(plan, where, cover, folded[0], parts)
+    return finish(plan, cover, folded[0], parts)
 
 
 def solution(mesh):

time: 63.3 us -> 53.9 us (0.85)
  Pallas kernels: 26.6 us -> 16.8 us
  waiting for transfers between devices: 12.8 us -> 13.6 us
    pallas_call x3, Pallas kernels: 19.2 us -> 14.3 us  [the longest x2 10.5 us: match(): pl.pallas_call(functools.partial(match_kernel, plan, first, images.shape[...]
    pallas_call x1, Pallas kernels: 2.26 us -> 0.1 us  [fold(): pl.pallas_call(fold_kernel, name='fold', in_specs=[vmem, vmem], out_specs...]
    pallas_call x1, Pallas kernels: 2.5 us -> 1.01 us  [cover_of(): pl.pallas_call(functools.partial(cover_kernel, plan), name='cover', in_sp...]
    pallas_call x1, Pallas kernels: 2.64 us -> 1.43 us  [finish(): pl.pallas_call(functools.partial(finish_kernel, plan, filt), name='finish...]
    ppermute x11, waiting for transfers between devices: 12.8 us -> 13.6 us  [swap(): lax.ppermute(value, axis, [(i, i ^ bit) for i in range(mesh.shape[axis])])]
    unnamed x36 -> x18, local copies, waits for them, and re-layouts: 4.96 us -> 5.31 us
  transfers between devices with their start and end apart: 11 -> 11, of which waited for: 4 -> 4; matrix products, arithmetic and copies ran while one was open for 0% -> 0% of each run, Pallas kernels for 15% -> 12%
where the time goes in v2:
time: 53.9 us; the launch traced here: 53.6 us
  starting transfers between devices  16.9 us (31%)
  Pallas kernels  16.8 us (31%)
  waiting for transfers between devices  13.6 us (25%)
  local copies, waits for them, and re-layouts  5.43 us (10%)
  between operations  0.77 us (1%)
    ppermute x11, starting transfers between devices, swap(): lax.ppermute(value, axis, [(i, i ^ bit) for i in range(mesh.shape[axis])])  16.9 us
    ppermute x11, waiting for transfers between devices, swap(): lax.ppermute(value, axis, [(i, i ^ bit) for i in range(mesh.shape[axis])])  13.6 us
    pallas_call x2, Pallas kernels, match(): pl.pallas_call(functools.partial(match_kernel, plan, first, images.shape[...  10.5 us
    unnamed x18, local copies, waits for them, and re-layouts  5.31 us
    pallas_call x1, Pallas kernels, place(): pl.pallas_call(functools.partial(place_kernel, plan, sizes, total), name=...  3.81 us
    pallas_call x1, Pallas kernels, finish(): pl.pallas_call(functools.partial(finish_kernel, plan, filt), name='finish...  1.43 us
  transfers between devices with their start and end apart: 11, of which 4 were waited for; matrix products, arithmetic and copies ran while one was open for 0% of the time, Pallas kernels for 12%

profile of v2, /device:TPU:0, one launch (start us, length us, event | category | flops | bytes accessed | tf_op | source)
XLA Modules:
  0.0 53.6 jit_solution(716425048774531600)
XLA Ops:
  0.6 0.0 copy-start
  0.6 1.2 %copy-done = bf16[256,2048]{1,0:T(8,128)(2,1)S(1)} copy-done((bf16[256,2048]{1,0:T(8,128)(2,1)S(1)}, bf16[256,2048]{1,0:T(8,128)(2,1)}, u32[]{:S(2)}) %copy-start) | copy-done | bytes 1048600
  1.9 0.0 copy-start.1
  1.9 1.1 %copy-done.1 = bf16[1,6,128,512]{3,2,1,0:T(8,128)(2,1)S(1)} copy-done((bf16[1,6,128,512]{3,2,1,0:T(8,128)(2,1)S(1)}, bf16[1,6,128,512]{3,2,1,0:T(8,128)(2,1)}, u32[]{:S(2)}) %copy-start.1) | copy-done | bytes 786456
  3.0 0.0 copy-start.2
  3.0 0.9 %copy-done.2 = f32[16,16,128]{2,1,0:T(8,128)S(1)} copy-done((f32[16,16,128]{2,1,0:T(8,128)S(1)}, f32[16,16,128]{2,1,0:T(8,128)}, u32[]{:S(2)}) %copy-start.2) | copy-done | bytes 131096
  3.9 0.0 copy-start.3
  3.9 0.7 %copy-done.3 = f32[1,6,3,40]{3,0,2,1:T(1,128)S(1)} copy-done((f32[1,6,3,40]{3,0,2,1:T(1,128)S(1)}, f32[1,6,3,40]{3,0,2,1:T(1,128)}, u32[]{:S(2)}) %copy-start.3) | copy-done | bytes 2904
  4.6 0.0 copy-start.4
  4.6 0.7 %copy-done.4 = f32[1,96,2]{1,2,0:T(2,128)S(1)} copy-done((f32[1,96,2]{1,2,0:T(2,128)S(1)}, f32[1,96,2]{1,2,0:T(2,128)}, u32[]{:S(2)}) %copy-start.4) | copy-done | bytes 792
  5.3 0.0 copy-start.5
  5.3 0.7 %copy-done.5 = s32[1,96]{1,0:T(1,128)S(1)} copy-done((s32[1,96]{1,0:T(1,128)S(1)}, s32[1,96]{1,0:T(1,128)}, u32[]{:S(2)}) %copy-start.5) | copy-done | bytes 408
  5.9 5.2 %match.2 = (bf16[3,72,512]{2,1,0:T(8,128)(2,1)S(1)}, bf16[3,72,512]{2,1,0:T(8,128)(2,1)S(1)}) custom-call(s32[1,96]{1,0:T(1,128)S(1)} %copy-done.5, f32[1,2,96]{2,1,0:T(2,128)S(1)} %bitcast.21, f32[6,3,1,40]{3,2,1,0:T(1,128)S(1)} %bitcast.19, bf16[1,6,128,512]{3,2,1,0:T(8,128)(2,1)S(1)} %copy-done.1, bf16[256,2048]{1,0:T(8,128)(2,1)S(1)} %copy-done, ...), custom_call_target="tpu_custom_call" | custom-call | tf_op jit(solution)/shard_map/match/pallas_call | solution.py:145
  11.2 0.0 copy-start.7
  11.2 0.0 copy-start.8
  11.2 0.0 copy-start.6
  11.2 3.0 %collective-permute-start.1 = (bf16[3,72,512]{2,1,0:T(8,128)(2,1)S(1)}, bf16[3,72,512]{2,1,0:T(8,128)(2,1)S(1)}, u32[]{:S(2)}, u32[]{:S(2)}) collective-permute-start(bf16[3,72,512]{2,1,0:T(8,128)(2,1)S(1)} %get-tuple-element.17), channel_id=1, source_target_pairs={{0,16},{16,0},{1,17},{17,1},{2,18},{18,2},{3,19},{19,3},{4,20},{20... | collective-permute-start | bytes 663560 | tf_op jit(solution)/shard_map/ppermute | solution.py:388
  14.2 5.2 %match.3 = (bf16[3,72,512]{2,1,0:T(8,128)(2,1)S(1)}, bf16[3,72,512]{2,1,0:T(8,128)(2,1)S(1)}) custom-call(s32[1,96]{1,0:T(1,128)S(1)} %copy-done.5, f32[1,2,96]{2,1,0:T(2,128)S(1)} %bitcast.22, f32[6,3,1,40]{3,2,1,0:T(1,128)S(1)} %bitcast.20, bf16[1,6,128,512]{3,2,1,0:T(8,128)(2,1)S(1)} %copy-done.1, bf16[256,2048]{1,0:T(8,128)(2,1)S(1)} %copy-done, ...), custom_call_target="tpu_custom_call" | custom-call | tf_op jit(solution)/shard_map/match/pallas_call | solution.py:145
  19.5 0.1 collective-permute-start.2
  19.6 0.0 copy-done.7
  19.6 0.0 copy-done.8
  19.6 0.0 copy-done.6
  19.7 0.1 copy.20.refs_0_
  19.8 2.1 %collective-permute-start = (f32[96,8]{1,0:T(8,128)S(1)}, f32[96,8]{1,0:T(8,128)S(1)}, u32[]{:S(2)}, u32[]{:S(2)}) collective-permute-start(f32[96,8]{1,0:T(8,128)S(1)} %copy.20.refs_0_), channel_id=1, source_target_pairs={{0,16},{16,0},{1,17},{17,1},{2,18},{18,2},{3,19},{19,3},{4,20},{20... | collective-permute-start | bytes 9224 | tf_op jit(solution)/shard_map/ppermute | solution.py:388
  21.8 5.7 %collective-permute-done.refs_1_ = f32[96,8]{1,0:T(8,128)S(1)} collective-permute-done((f32[96,8]{1,0:T(8,128)S(1)}, f32[96,8]{1,0:T(8,128)S(1)}, u32[]{:S(2)}, u32[]{:S(2)}) %collective-permute-start) | collective-permute-done | bytes 3104 | tf_op jit(solution)/shard_map/ppermute | solution.py:388
  27.5 0.0 collective-permute-done.1.refs_3_
  27.5 0.0 collective-permute-done.2.refs_5_
  27.5 3.8 %place.1 = (bf16[8,72,512]{2,1,0:T(8,128)(2,1)S(1)}, f32[8,72,512]{2,1,0:T(8,128)S(1)}) custom-call(f32[96,8]{1,0:T(8,128)S(1)} %copy.20.refs_0_, f32[96,8]{1,0:T(8,128)S(1)} %collective-permute-done.refs_1_, bf16[3,72,512]{2,1,0:T(8,128)(2,1)S(1)} %get-tuple-element.16.refs_2_, bf16[3,72,512]{2,1,0:T(8,128)(2,1)S(1)} %collective-permute-done.1.refs_3_, ...), custom_call_target="tpu_custom_call" | custom-call | tf_op jit(solution)/shard_map/place/pallas_call | solution.py:226
  31.3 0.1 collective-permute-start.3
  31.4 2.0 %collective-permute-done.3.got_ref = bf16[8,72,512]{2,1,0:T(8,128)(2,1)S(1)} collective-permute-done((bf16[8,72,512]{2,1,0:T(8,128)(2,1)S(1)}, bf16[8,72,512]{2,1,0:T(8,128)(2,1)S(1)}, u32[]{:S(2)}, u32[]{:S(2)}) %collective-permute-start.3) | collective-permute-done | bytes 589856 | tf_op jit(solution)/shard_map/ppermute | solution.py:388
  33.4 0.1 fold.1
  33.5 4.6 %collective-permute-start.10 = (bf16[72,512]{1,0:T(8,128)(2,1)S(1)}, bf16[72,512]{1,0:T(8,128)(2,1)S(1)}, u32[]{:S(2)}, u32[]{:S(2)}) collective-permute-start(bf16[72,512]{1,0:T(8,128)(2,1)S(1)} %get-tuple-element.29), channel_id=1, source_target_pairs={{0,14},{1,15},{2,12},{3,13},{4,10},{5,11},{6,8},{7,9},{8,6},{9,7},... | collective-permute-start | bytes 221192 | tf_op jit(solution)/shard_map/ppermute | solution.py:388
  38.1 0.5 collective-permute-start.4
  38.6 0.0 collective-permute-start.5
  38.6 3.0 %collective-permute-start.6 = (bf16[72,512]{1,0:T(8,128)(2,1)S(1)}, bf16[72,512]{1,0:T(8,128)(2,1)S(1)}, u32[]{:S(2)}, u32[]{:S(2)}) collective-permute-start(bf16[72,512]{1,0:T(8,128)(2,1)S(1)} %get-tuple-element.25), channel_id=1, source_target_pairs={{0,6},{1,7},{2,4},{3,5},{4,2},{5,3},{6,0},{7,1},{8,14},{9,15},{10,... | collective-permute-start | bytes 221192 | tf_op jit(solution)/shard_map/ppermute | solution.py:388
  41.6 0.0 collective-permute-start.7
  41.6 0.0 collective-permute-done.10.refs_6_
  41.6 2.9 %collective-permute-start.8 = (bf16[72,512]{1,0:T(8,128)(2,1)S(1)}, bf16[72,512]{1,0:T(8,128)(2,1)S(1)}, u32[]{:S(2)}, u32[]{:S(2)}) collective-permute-start(bf16[72,512]{1,0:T(8,128)(2,1)S(1)} %get-tuple-element.27), channel_id=1, source_target_pairs={{0,10},{1,11},{2,8},{3,9},{4,14},{5,15},{6,12},{7,13},{8,2},{9,3},... | collective-permute-start | bytes 221192 | tf_op jit(solution)/shard_map/ppermute | solution.py:388
  44.4 0.0 collective-permute-done.4.refs_0_
  44.4 0.7 %collective-permute-start.9 = (bf16[72,512]{1,0:T(8,128)(2,1)S(1)}, bf16[72,512]{1,0:T(8,128)(2,1)S(1)}, u32[]{:S(2)}, u32[]{:S(2)}) collective-permute-start(bf16[72,512]{1,0:T(8,128)(2,1)S(1)} %get-tuple-element.28), channel_id=1, source_target_pairs={{0,12},{1,13},{2,14},{3,15},{4,8},{5,9},{6,10},{7,11},{8,4},{9,5},... | collective-permute-start | bytes 221192 | tf_op jit(solution)/shard_map/ppermute | solution.py:388
  45.2 1.0 %cover.1.cover_ref = f32[72,512]{1,0:T(8,128)S(1)} custom-call(f32[96,8]{1,0:T(8,128)S(1)} %copy.20.refs_0_, f32[96,8]{1,0:T(8,128)S(1)} %collective-permute-done.refs_1_), custom_call_target="tpu_custom_call" | custom-call | tf_op jit(solution)/shard_map/cover/pallas_call | solution.py:296
  46.2 0.0 collective-permute-done.5.refs_1_
  46.2 0.0 collective-permute-done.6.refs_2_
  46.2 3.5 %collective-permute-done.7.refs_3_ = bf16[72,512]{1,0:T(8,128)(2,1)S(1)} collective-permute-done((bf16[72,512]{1,0:T(8,128)(2,1)S(1)}, bf16[72,512]{1,0:T(8,128)(2,1)S(1)}, u32[]{:S(2)}, u32[]{:S(2)}) %collective-permute-start.7) | collective-permute-done | bytes 73760 | tf_op jit(solution)/shard_map/ppermute | solution.py:388
  49.7 2.4 %collective-permute-done.8.refs_4_ = bf16[72,512]{1,0:T(8,128)(2,1)S(1)} collective-permute-done((bf16[72,512]{1,0:T(8,128)(2,1)S(1)}, bf16[72,512]{1,0:T(8,128)(2,1)S(1)}, u32[]{:S(2)}, u32[]{:S(2)}) %collective-permute-start.8) | collective-permute-done | bytes 73760 | tf_op jit(solution)/shard_map/ppermute | solution.py:388
  52.2 0.0 collective-permute-done.9.refs_5_
  52.2 1.4 %finish.1 = (f32[64,512]{1,0:T(8,128)}, f32[64,512]{1,0:T(8,128)}) custom-call(f32[72,512]{1,0:T(8,128)S(1)} %cover.1.cover_ref, f32[72,512]{1,0:T(8,128)S(1)} %get-tuple-element.22.own_ref, bf16[72,512]{1,0:T(8,128)(2,1)S(1)} %collective-permute-done.4.refs_0_, bf16[72,512]{1,0:T(8,128)(2,1)S(1)} %collective-permute-done.5.refs_1_, ...), custom_call_target="tpu_custom_call" | custom-call | tf_op jit(solution)/shard_map/finish/pallas_call | solution.py:350
  (5 shorter events, 0.0 us)
Async XLA Ops:
  0.6 1.2 %copy-start = (bf16[256,2048]{1,0:T(8,128)(2,1)S(1)}, bf16[256,2048]{1,0:T(8,128)(2,1)}, u32[]{:S(2)}) copy-start(bf16[256,2048]{1,0:T(8,128)(2,1)} %constant.10.clone.table_ref) | copy-start | bytes 3145732
  1.9 1.1 %copy-start.1 = (bf16[1,6,128,512]{3,2,1,0:T(8,128)(2,1)S(1)}, bf16[1,6,128,512]{3,2,1,0:T(8,128)(2,1)}, u32[]{:S(2)}) copy-start(bf16[1,6,128,512]{3,2,1,0:T(8,128)(2,1)} %image_ref.3) | copy-start | bytes 2359300
  3.0 0.9 %copy-start.2 = (f32[16,16,128]{2,1,0:T(8,128)S(1)}, f32[16,16,128]{2,1,0:T(8,128)}, u32[]{:S(2)}) copy-start(f32[16,16,128]{2,1,0:T(8,128)} %constant.11.clone.tap_ref) | copy-start | bytes 393220
  3.9 0.7 %copy-start.3 = (f32[1,6,3,40]{3,0,2,1:T(1,128)S(1)}, f32[1,6,3,40]{3,0,2,1:T(1,128)}, u32[]{:S(2)}) copy-start(f32[1,6,3,40]{3,0,2,1:T(1,128)} %param.10) | copy-start | bytes 8644
  4.6 0.7 %copy-start.4 = (f32[1,96,2]{1,2,0:T(2,128)S(1)}, f32[1,96,2]{1,2,0:T(2,128)}, u32[]{:S(2)}) copy-start(f32[1,96,2]{1,2,0:T(2,128)} %param.14) | copy-start | bytes 2308
  5.3 0.7 %copy-start.5 = (s32[1,96]{1,0:T(1,128)S(1)}, s32[1,96]{1,0:T(1,128)}, u32[]{:S(2)}) copy-start(s32[1,96]{1,0:T(1,128)} %row_ref.3) | copy-start | bytes 1156
  11.2 8.4 %copy-start.7 = (s32[1,96,2]{1,2,0:T(2,128)S(1)}, s32[1,96,2]{1,2,0:T(2,128)}, u32[]{:S(2)}) copy-start(s32[1,96,2]{1,2,0:T(2,128)} %param.11) | copy-start | bytes 2308
  11.2 8.4 %copy-start.8 = (s32[1,96]{1,0:T(1,128)S(1)}, s32[1,96]{1,0:T(1,128)}, u32[]{:S(2)}) copy-start(s32[1,96]{1,0:T(1,128)} %param.13) | copy-start | bytes 1156
  11.2 8.4 %copy-start.6 = (f32[1,96]{1,0:T(1,128)S(1)}, f32[1,96]{1,0:T(1,128)}, u32[]{:S(2)}) copy-start(f32[1,96]{1,0:T(1,128)} %param.15) | copy-start | bytes 1156
  11.2 16.3 %collective-permute-start.1 = (bf16[3,72,512]{2,1,0:T(8,128)(2,1)S(1)}, bf16[3,72,512]{2,1,0:T(8,128)(2,1)S(1)}, u32[]{:S(2)}, u32[]{:S(2)}) collective-permute-start(bf16[3,72,512]{2,1,0:T(8,128)(2,1)S(1)} %get-tuple-element.17), channel_id=1, source_target_pairs={{0,16},{16,0},{1,17},{17,1},{2,18},{18,2},{3,19},{19,3},{4,20},{20... | collective-permute-start | bytes 663560 | tf_op jit(solution)/shard_map/ppermute | solution.py:388
  19.5 8.0 %collective-permute-start.2 = (bf16[3,72,512]{2,1,0:T(8,128)(2,1)S(1)}, bf16[3,72,512]{2,1,0:T(8,128)(2,1)S(1)}, u32[]{:S(2)}, u32[]{:S(2)}) collective-permute-start(bf16[3,72,512]{2,1,0:T(8,128)(2,1)S(1)} %get-tuple-element.19), channel_id=1, source_target_pairs={{0,16},{16,0},{1,17},{17,1},{2,18},{18,2},{3,19},{19,3},{4,20},{20... | collective-permute-start | bytes 663560 | tf_op jit(solution)/shard_map/ppermute | solution.py:388
  19.8 7.7 %collective-permute-start = (f32[96,8]{1,0:T(8,128)S(1)}, f32[96,8]{1,0:T(8,128)S(1)}, u32[]{:S(2)}, u32[]{:S(2)}) collective-permute-start(f32[96,8]{1,0:T(8,128)S(1)} %copy.20.refs_0_), channel_id=1, source_target_pairs={{0,16},{16,0},{1,17},{17,1},{2,18},{18,2},{3,19},{19,3},{4,20},{20... | collective-permute-start | bytes 9224 | tf_op jit(solution)/shard_map/ppermute | solution.py:388
  31.3 2.1 %collective-permute-start.3 = (bf16[8,72,512]{2,1,0:T(8,128)(2,1)S(1)}, bf16[8,72,512]{2,1,0:T(8,128)(2,1)S(1)}, u32[]{:S(2)}, u32[]{:S(2)}) collective-permute-start(bf16[8,72,512]{2,1,0:T(8,128)(2,1)S(1)} %get-tuple-element.21), channel_id=1, source_target_pairs={{0,1},{1,0},{2,3},{3,2},{4,5},{5,4},{6,7},{7,6},{8,9},{9,8},{10,11... | collective-permute-start | bytes 1769480 | tf_op jit(solution)/shard_map/ppermute | solution.py:388
  33.5 8.1 %collective-permute-start.10 = (bf16[72,512]{1,0:T(8,128)(2,1)S(1)}, bf16[72,512]{1,0:T(8,128)(2,1)S(1)}, u32[]{:S(2)}, u32[]{:S(2)}) collective-permute-start(bf16[72,512]{1,0:T(8,128)(2,1)S(1)} %get-tuple-element.29), channel_id=1, source_target_pairs={{0,14},{1,15},{2,12},{3,13},{4,10},{5,11},{6,8},{7,9},{8,6},{9,7},... | collective-permute-start | bytes 221192 | tf_op jit(solution)/shard_map/ppermute | solution.py:388
  38.1 6.4 %collective-permute-start.4 = (bf16[72,512]{1,0:T(8,128)(2,1)S(1)}, bf16[72,512]{1,0:T(8,128)(2,1)S(1)}, u32[]{:S(2)}, u32[]{:S(2)}) collective-permute-start(bf16[72,512]{1,0:T(8,128)(2,1)S(1)} %get-tuple-element.23), channel_id=1, source_target_pairs={{0,2},{1,3},{2,0},{3,1},{4,6},{5,7},{6,4},{7,5},{8,10},{9,11},{10,... | collective-permute-start | bytes 221192 | tf_op jit(solution)/shard_map/ppermute | solution.py:388
  38.6 7.6 %collective-permute-start.5 = (bf16[72,512]{1,0:T(8,128)(2,1)S(1)}, bf16[72,512]{1,0:T(8,128)(2,1)S(1)}, u32[]{:S(2)}, u32[]{:S(2)}) collective-permute-start(bf16[72,512]{1,0:T(8,128)(2,1)S(1)} %get-tuple-element.24), channel_id=1, source_target_pairs={{0,4},{1,5},{2,6},{3,7},{4,0},{5,1},{6,2},{7,3},{8,12},{9,13},{10,... | collective-permute-start | bytes 221192 | tf_op jit(solution)/shard_map/ppermute | solution.py:388
  38.6 7.6 %collective-permute-start.6 = (bf16[72,512]{1,0:T(8,128)(2,1)S(1)}, bf16[72,512]{1,0:T(8,128)(2,1)S(1)}, u32[]{:S(2)}, u32[]{:S(2)}) collective-permute-start(bf16[72,512]{1,0:T(8,128)(2,1)S(1)} %get-tuple-element.25), channel_id=1, source_target_pairs={{0,6},{1,7},{2,4},{3,5},{4,2},{5,3},{6,0},{7,1},{8,14},{9,15},{10,... | collective-permute-start | bytes 221192 | tf_op jit(solution)/shard_map/ppermute | solution.py:388
  41.6 8.2 %collective-permute-start.7 = (bf16[72,512]{1,0:T(8,128)(2,1)S(1)}, bf16[72,512]{1,0:T(8,128)(2,1)S(1)}, u32[]{:S(2)}, u32[]{:S(2)}) collective-permute-start(bf16[72,512]{1,0:T(8,128)(2,1)S(1)} %get-tuple-element.26), channel_id=1, source_target_pairs={{0,8},{1,9},{2,10},{3,11},{4,12},{5,13},{6,14},{7,15},{8,0},{9,1},... | collective-permute-start | bytes 221192 | tf_op jit(solution)/shard_map/ppermute | solution.py:388
  41.6 10.6 %collective-permute-start.8 = (bf16[72,512]{1,0:T(8,128)(2,1)S(1)}, bf16[72,512]{1,0:T(8,128)(2,1)S(1)}, u32[]{:S(2)}, u32[]{:S(2)}) collective-permute-start(bf16[72,512]{1,0:T(8,128)(2,1)S(1)} %get-tuple-element.27), channel_id=1, source_target_pairs={{0,10},{1,11},{2,8},{3,9},{4,14},{5,15},{6,12},{7,13},{8,2},{9,3},... | collective-permute-start | bytes 221192 | tf_op jit(solution)/shard_map/ppermute | solution.py:388
  44.4 7.7 %collective-permute-start.9 = (bf16[72,512]{1,0:T(8,128)(2,1)S(1)}, bf16[72,512]{1,0:T(8,128)(2,1)S(1)}, u32[]{:S(2)}, u32[]{:S(2)}) collective-permute-start(bf16[72,512]{1,0:T(8,128)(2,1)S(1)} %get-tuple-element.28), channel_id=1, source_target_pairs={{0,12},{1,13},{2,14},{3,15},{4,8},{5,9},{6,10},{7,11},{8,4},{9,5},... | collective-permute-start | bytes 221192 | tf_op jit(solution)/shard_map/ppermute | solution.py:388

commit v3 on v2

--- a/solution.py
+++ b/solution.py
@@ -63,137 +63,195 @@
             self.useful = self.block + 2 * DRAD
             self.step, self.first = self.block, -DRAD
         self.rows = -(-(self.useful + 4) // 8) * 8
+        self.near = self.patches // 4
 
     def base(self, visit):
         return visit * self.step + self.first
 
 
-def match_kernel(plan, first, total, row_ref, shift_ref, coef_ref, image_ref, table_ref, tap_ref, *rest):
-    outs, (grid_ref, left_ref) = rest[:-2], rest[-2:]
-    step = pl.program_id(0)
-    ccd = first + step
-    visit = lax.axis_index("visit")
-    index = lax.axis_index("patch") * total + ccd
+def match_kernel(plan, first, total, fetch, *refs):
+    ins, rest = refs[:6], refs[6:]
+    outs, rest = rest[: plan.visits], rest[plan.visits :]
+    window_ref, grid_ref, left_ref = rest[:3]
     height, width = plan.height, plan.width
     tiles = width // LANE
-
-    image = image_ref[0, 0]
-    edge = jnp.zeros((height, LANE // 2), image.dtype)
-    padded = jnp.concatenate([edge, image, edge], axis=1)
-    for pair in range(8):
-        table = table_ref[:, pair * 256 : (pair + 1) * 256]
-        for t in range(tiles):
-            out = jnp.dot(padded[:, t * LANE : (t + 2) * LANE], table, preferred_element_type=jnp.float32)
-            out = out.astype(jnp.bfloat16)
-            for half in range(2):
-                g = pair * 2 + half
-                grid_ref[g * height : (g + 1) * height, t * LANE : (t + 1) * LANE] = out[:, half * LANE : (half + 1) * LANE]
-
+    count = outs[0].shape[0]
+    if fetch:
+        homes, sems = rest[3:9], rest[9]
+        copies = []
+        for n in (2, 5, 3, 4, 0, 1):
+            source = ins[n].at[:, pl.ds(first, count)] if n == 3 else ins[n]
+            copies.append((n, pltpu.make_async_copy(source, homes[n], sems.at[n])))
+        for n, copy in copies:
+            copy.start()
+        ins, base = homes, 0
+        arrive = {n: copy.wait for n, copy in copies}
+    else:
+        base = first
+        arrive = {n: lambda: None for n in range(6)}
+    row_ref, shift_ref, coef_ref, image_ref, table_ref, tap_ref = ins
+
+    arrive[2]()
+    arrive[5]()
     local_row = iota((16, LANE), 0).astype(jnp.float32)
     lane = iota((16, LANE), 1)
     yn = (2.0 * local_row + 1.0) / height - 1.0
-    for g, (s, i) in enumerate(PAIRS):
-        term = s * 10 + (0, 4, 7, 9)[i]
-        sums = []
-        for q in range(3):
-            total = coef_ref[ccd, q, 0, term] * tap_ref[s * 4]
-            for j in range(1, 4 - i):
-                total = total + coef_ref[ccd, q, 0, term + j] * tap_ref[s * 4 + j]
-            sums.append(total)
-        steady = sums[0] + yn * sums[1]
-        flat = sums[2].astype(jnp.bfloat16)
-        for b in range(height // 16):
-            tall = (steady + (32.0 * b / height) * sums[1]).astype(jnp.bfloat16)
-            wide = flat
-            if b:
-                tall = pltpu.roll(tall, 16 * b, 1)
-                wide = pltpu.roll(wide, 16 * b, 1)
-            if b == 0:
-                tall = jnp.where(lane < LANE // 2, tall, jnp.zeros_like(tall))
-                wide = jnp.where(lane < LANE // 2, wide, jnp.zeros_like(wide))
-            if b == height // 16 - 1:
-                tall = jnp.where(lane >= LANE // 2, tall, jnp.zeros_like(tall))
-                wide = jnp.where(lane >= LANE // 2, wide, jnp.zeros_like(wide))
-            left_ref[16 * b : 16 * b + 16, g * LANE : (g + 1) * LANE] = tall
-            left_ref[height + 16 * b : height + 16 * b + 16, g * LANE : (g + 1) * LANE] = wide
-
-    both = jnp.dot(left_ref[...], grid_ref[...], preferred_element_type=jnp.float32)
-    xn = (2.0 * iota((height, width), 1).astype(jnp.float32) + 1.0) / width - 1.0
-    matched = (both[:height] + xn * both[height:]).astype(jnp.bfloat16)
-
-    shift = row_ref[0, index]
-    frac = jnp.full((plan.rows, height), shift_ref[0, 0, index], jnp.float32)
-    upper = (1.0 - frac).astype(jnp.bfloat16)
-    lower = frac.astype(jnp.bfloat16)
+
+    def coefficients(e):
+        for g, (s, i) in enumerate(PAIRS):
+            term = s * 10 + (0, 4, 7, 9)[i]
+            sums = []
+            for q in range(3):
+                total_tap = coef_ref[first + e, q, 0, term] * tap_ref[s * 4]
+                for j in range(1, 4 - i):
+                    total_tap = total_tap + coef_ref[first + e, q, 0, term + j] * tap_ref[s * 4 + j]
+                sums.append(total_tap)
+            steady = sums[0] + yn * sums[1]
+            flat = sums[2].astype(jnp.bfloat16)
+            for b in range(height // 16):
+                tall = (steady + (32.0 * b / height) * sums[1]).astype(jnp.bfloat16)
+                wide = flat
+                if b:
+                    tall = pltpu.roll(tall, 16 * b, 1)
+                    wide = pltpu.roll(wide, 16 * b, 1)
+                if b == 0:
+                    tall = jnp.where(lane < LANE // 2, tall, jnp.zeros_like(tall))
+                    wide = jnp.where(lane < LANE // 2, wide, jnp.zeros_like(wide))
+                if b == height // 16 - 1:
+                    tall = jnp.where(lane >= LANE // 2, tall, jnp.zeros_like(tall))
+                    wide = jnp.where(lane >= LANE // 2, wide, jnp.zeros_like(wide))
+                left_ref[e, 16 * b : 16 * b + 16, g * LANE : (g + 1) * LANE] = tall
+                left_ref[e, height + 16 * b : height + 16 * b + 16, g * LANE : (g + 1) * LANE] = wide
+
+    coefficients(0)
+    arrive[3]()
+    edge = jnp.zeros((height, LANE // 2), jnp.bfloat16)
+    for e in range(count):
+        padded = jnp.concatenate([edge, image_ref[0, base + e], edge], axis=1)
+        for t in range(tiles):
+            spot = (e * tiles + t) * height
+            window_ref[spot : spot + height] = padded[:, t * LANE : (t + 2) * LANE]
+    arrive[4]()
+    for pair in range(8):
+        out = jnp.dot(window_ref[...], table_ref[:, pair * 256 : (pair + 1) * 256], preferred_element_type=jnp.float32)
+        out = out.astype(jnp.bfloat16)
+        for e in range(count):
+            for t in range(tiles):
+                spot = (e * tiles + t) * height
+                for half in range(2):
+                    g = pair * 2 + half
+                    grid_ref[e, g * height : (g + 1) * height, t * LANE : (t + 1) * LANE] = out[
+                        spot : spot + height, half * LANE : (half + 1) * LANE
+                    ]
+    for e in range(1, count):
+        coefficients(e)
+    arrive[0]()
+    arrive[1]()
+    visit = lax.axis_index("visit")
     local = iota((plan.rows, height), 0)
     source = iota((plan.rows, height), 1)
-    nothing = jnp.zeros_like(upper)
-    for d, out_ref in enumerate(outs):
-        sky = local + plan.base(visit ^ d)
-        good = (local < plan.useful) & (sky >= 0) & (sky < height)
-        gap = jnp.where(good, source - sky + shift, 2 * height)
-        rows = jnp.where(gap == 0, upper, jnp.where(gap == -1, lower, nothing))
-        warped = jnp.dot(rows, matched, preferred_element_type=jnp.float32)
-        out_ref[0] = warped.astype(jnp.bfloat16)
-
-
-def match(plan, chunk, row_offset, shifts, coefficients, images, table, taps):
+    xn = (2.0 * iota((height, width), 1).astype(jnp.float32) + 1.0) / width - 1.0
+    for e in range(count):
+        index = lax.axis_index("patch") * total + first + e
+        both = jnp.dot(left_ref[e], grid_ref[e], preferred_element_type=jnp.float32)
+        matched = (both[:height] + xn * both[height:]).astype(jnp.bfloat16)
+        shift = row_ref[0, index]
+        frac = jnp.full((plan.rows, height), shift_ref[0, 0, index], jnp.float32)
+        upper = (1.0 - frac).astype(jnp.bfloat16)
+        lower = frac.astype(jnp.bfloat16)
+        nothing = jnp.zeros_like(upper)
+        for d, out_ref in enumerate(outs):
+            sky = local + plan.base(visit ^ d)
+            good = (local < plan.useful) & (sky >= 0) & (sky < height)
+            gap = jnp.where(good, source - sky + shift, 2 * height)
+            rows = jnp.where(gap == 0, upper, jnp.where(gap == -1, lower, nothing))
+            warped = jnp.dot(rows, matched, preferred_element_type=jnp.float32)
+            out_ref[e] = warped.astype(jnp.bfloat16)
+
+
+def match(plan, chunk, fetch, row_offset, shifts, coefficients, images, table, taps):
     first, last = chunk
     count = last - first
-    smem = pl.BlockSpec(memory_space=pltpu.SMEM)
     height, width = plan.height, plan.width
-    return pl.pallas_call(
-        functools.partial(match_kernel, plan, first, images.shape[1]),
+    operands = (row_offset, shifts, coefficients, images, table, taps)
+    spaces = [pltpu.SMEM] * 3 + [pltpu.VMEM] * 3
+    scratch = [
+        pltpu.VMEM((count * 4 * height, 2 * LANE), jnp.bfloat16),
+        pltpu.VMEM((count, 16 * height, width), jnp.bfloat16),
+        pltpu.VMEM((count, 2 * height, 16 * LANE), jnp.bfloat16),
+    ]
+    if fetch:
+        for n, (operand, space) in enumerate(zip(operands, spaces)):
+            shape = (1, count) + operand.shape[2:] if n == 3 else operand.shape
+            scratch.append(space(shape, operand.dtype))
+        scratch.append(pltpu.SemaphoreType.DMA((6,)))
+        spaces = [pltpu.HBM] * 6
+    return pl.pallas_call(
+        functools.partial(match_kernel, plan, first, images.shape[1], fetch),
         name="match",
-        grid=(count,),
-        in_specs=[
-            smem,
-            smem,
-            smem,
-            pl.BlockSpec((1, 1, height, width), lambda e: (0, first + e, 0, 0)),
-            pl.BlockSpec(table.shape, lambda e: (0, 0)),
-            pl.BlockSpec(taps.shape, lambda e: (0, 0, 0)),
-        ],
-        out_specs=[pl.BlockSpec((1, plan.rows, width), lambda e: (e, 0, 0))] * plan.visits,
+        in_specs=[pl.BlockSpec(memory_space=space) for space in spaces],
+        out_specs=[pl.BlockSpec(memory_space=pltpu.VMEM)] * plan.visits,
         out_shape=[jax.ShapeDtypeStruct((count, plan.rows, width), jnp.bfloat16)] * plan.visits,
-        scratch_shapes=[
-            pltpu.VMEM((16 * height, width), jnp.bfloat16),
-            pltpu.VMEM((2 * height, 16 * LANE), jnp.bfloat16),
-        ],
-        compiler_params=pltpu.CompilerParams(vmem_limit_bytes=20 * MIB),
-    )(row_offset, shifts, coefficients, images, table, taps)
-
-
-def place_kernel(plan, sizes, total, *refs):
-    metas = refs[: plan.visits]
-    sources = refs[plan.visits : -3]
-    send_ref, keep_ref, strip_ref = refs[-3:]
+        scratch_shapes=scratch,
+        compiler_params=pltpu.CompilerParams(vmem_limit_bytes=61 * MIB),
+    )(*operands)
+
+
+def place_one(plan, strip_ref, gap, meta_ref, index, source):
     rows, width = plan.rows, plan.width
+    tiles = width // LANE
+    blank = jnp.zeros((rows, LANE), jnp.bfloat16)
+    nothing = jnp.zeros(gap.shape, jnp.bfloat16)
+    start = meta_ref[index, 0].astype(jnp.int32)
+    rem = start & (LANE - 1)
+    tile = (start >> 7) + 1
+    left = jnp.full(gap.shape, meta_ref[index, 2], jnp.float32).astype(jnp.bfloat16)
+    right = jnp.full(gap.shape, meta_ref[index, 3], jnp.float32).astype(jnp.bfloat16)
+    table = jnp.where(gap == -rem, left, jnp.where(gap == -rem - 1, right, nothing))
+    source = jnp.concatenate([blank, source, blank], axis=1)
+    windows = jnp.concatenate([source[:, t * LANE : (t + 2) * LANE] for t in range(tiles + 1)], axis=0)
+    out = jnp.dot(windows, table, preferred_element_type=jnp.float32)
+    weight = meta_ref[index, 6]
+    for t in range(tiles + 1):
+        strip_ref[tile + t] = strip_ref[tile + t] + weight * out[t * rows : (t + 1) * rows]
+
+
+def place_all(plan, strip_ref, total, metas, jobs, sources):
     patch = lax.axis_index("patch")
+    gap = iota((2 * LANE, LANE), 0) - iota((2 * LANE, LANE), 1) - LANE
+    for (d, first, last), source_ref in zip(jobs, sources):
+        for k in range(last - first):
+            place_one(plan, strip_ref, gap, metas[d], patch * total + first + k, source_ref[k])
+
+
+def early_kernel(plan, jobs, total, *refs):
+    metas, sources, strip_ref = refs[: plan.visits], refs[plan.visits : -1], refs[-1]
     strip_ref[...] = jnp.zeros_like(strip_ref)
-    gap = iota((2 * LANE, LANE), 0) - iota((2 * LANE, LANE), 1) - LANE
-    nothing = jnp.zeros((2 * LANE, LANE), jnp.bfloat16)
-    blank = jnp.zeros((rows, LANE), jnp.bfloat16)
+    place_all(plan, strip_ref, total, metas, jobs, sources)
+
+
+def early(plan, jobs, total, metas, sources):
+    vmem = pl.BlockSpec(memory_space=pltpu.VMEM)
+    shape = (plan.patches * plan.width // LANE + 2, plan.rows, LANE)
+    return pl.pallas_call(
+        functools.partial(early_kernel, plan, jobs, total),
+        name="early",
+        in_specs=[pl.BlockSpec(memory_space=pltpu.SMEM)] * plan.visits + [vmem] * len(sources),
+        out_specs=vmem,
+        out_shape=jax.ShapeDtypeStruct(shape, jnp.float32),
+        compiler_params=pltpu.CompilerParams(vmem_limit_bytes=16 * MIB),
+    )(*metas, *sources)
+
+
+def late_kernel(plan, jobs, total, *refs):
+    metas, rest = refs[: plan.visits], refs[plan.visits :]
+    sources, rest = rest[: len(jobs)], rest[len(jobs) + 1 :]
+    strip_ref, send_far, send_near, keep_far, keep_near = rest
+    place_all(plan, strip_ref, total, metas, jobs, sources)
+
+    rows, width = plan.rows, plan.width
     tiles = width // LANE
-    spot = 0
-    for first, last in sizes:
-        for d in range(plan.visits):
-            meta_ref, source_ref = metas[d], sources[spot]
-            spot += 1
-            for k in range(last - first):
-                index = patch * total + first + k
-                start = meta_ref[index, 0].astype(jnp.int32)
-                rem = start & (LANE - 1)
-                tile = (start >> 7) + 1
-                left = jnp.full(nothing.shape, meta_ref[index, 2], jnp.float32).astype(jnp.bfloat16)
-                right = jnp.full(nothing.shape, meta_ref[index, 3], jnp.float32).astype(jnp.bfloat16)
-                table = jnp.where(gap == -rem, left, jnp.where(gap == -rem - 1, right, nothing))
-                source = jnp.concatenate([blank, source_ref[k], blank], axis=1)
-                weight = meta_ref[index, 6]
-                for t in range(tiles + 1):
-                    out = jnp.dot(source[:, t * LANE : (t + 2) * LANE], table, preferred_element_type=jnp.float32)
-                    strip_ref[tile + t] = strip_ref[tile + t] + weight * out
-
+    patch = lax.axis_index("patch")
     core = patch & 1
     chip = patch >> 1
     pick = iota((8, LANE), 0) - 4
@@ -205,36 +263,40 @@
         out = lax.dot_general(table, block.astype(jnp.bfloat16), (((1,), (1,)), ((), ())), preferred_element_type=jnp.float32)
         return jnp.pad(out, ((0, 0), (0, LANE - rows)))
 
-    def emit(m, parity, out_ref):
+    def emit(m, parity, out_ref, spot):
         tile = (2 * (chip ^ m) + parity) * tiles + 1
         sides = (across(pick_left, strip_ref[tile - 1]), across(pick_right, strip_ref[tile + tiles]))
         for t in range(tiles):
             body = strip_ref[tile + t]
             if t < 2:
                 body = jnp.concatenate([body[: rows - 8], body[rows - 8 :] + sides[t]], axis=0)
-            out_ref[m, :, t * LANE : (t + 1) * LANE] = body.astype(out_ref.dtype)
-
-    for m in range(plan.patches // 2):
-        emit(m, 1 - core, send_ref)
-        emit(m, core, keep_ref)
-
-
-def place(plan, sizes, total, metas, sources):
-    smem = pl.BlockSpec(memory_space=pltpu.SMEM)
+            out_ref[spot, :, t * LANE : (t + 1) * LANE] = body.astype(out_ref.dtype)
+
+    near = plan.near
+    for m in range(near, 2 * near):
+        emit(m, 1 - core, send_far, m - near)
+    for m in range(near):
+        emit(m, 1 - core, send_near, m)
+    for m in range(near, 2 * near):
+        emit(m, core, keep_far, m - near)
+    for m in range(near):
+        emit(m, core, keep_near, m)
+
+
+def late(plan, jobs, total, metas, sources, strip):
     vmem = pl.BlockSpec(memory_space=pltpu.VMEM)
-    half = plan.patches // 2
-    return pl.pallas_call(
-        functools.partial(place_kernel, plan, sizes, total),
-        name="place",
-        in_specs=[smem] * plan.visits + [vmem] * len(sources),
-        out_specs=[vmem, vmem],
-        out_shape=[
-            jax.ShapeDtypeStruct((half, plan.rows, plan.width), jnp.bfloat16),
-            jax.ShapeDtypeStruct((half, plan.rows, plan.width), jnp.float32),
-        ],
-        scratch_shapes=[pltpu.VMEM((plan.patches * plan.width // LANE + 2, plan.rows, LANE), jnp.float32)],
+    shape = (plan.near, plan.rows, plan.width)
+    outs = [jax.ShapeDtypeStruct(strip.shape, strip.dtype)]
+    outs += [jax.ShapeDtypeStruct(shape, jnp.bfloat16)] * 2 + [jax.ShapeDtypeStruct(shape, jnp.float32)] * 2
+    return pl.pallas_call(
+        functools.partial(late_kernel, plan, jobs, total),
+        name="late",
+        in_specs=[pl.BlockSpec(memory_space=pltpu.SMEM)] * plan.visits + [vmem] * (len(sources) + 1),
+        out_specs=[vmem] * 5,
+        out_shape=outs,
+        input_output_aliases={plan.visits + len(sources): 0},
         compiler_params=pltpu.CompilerParams(vmem_limit_bytes=16 * MIB),
-    )(*metas, *sources)
+    )(*metas, *sources, strip)[1:]
 
 
 def fold_kernel(keep_ref, got_ref, *outs):
@@ -242,17 +304,17 @@
         out_ref[...] = (keep_ref[m] + got_ref[m].astype(jnp.float32)).astype(out_ref.dtype)
 
 
-def fold(plan, keep, got):
+def fold(plan, keep, got, own):
     vmem = pl.BlockSpec(memory_space=pltpu.VMEM)
-    half = plan.patches // 2
     shape = (plan.rows, plan.width)
+    types = [jnp.float32 if own and m == 0 else jnp.bfloat16 for m in range(plan.near)]
     return pl.pallas_call(
         fold_kernel,
         name="fold",
         in_specs=[vmem, vmem],
-        out_specs=[vmem] * half,
-        out_shape=[jax.ShapeDtypeStruct(shape, jnp.float32)] + [jax.ShapeDtypeStruct(shape, jnp.bfloat16)] * (half - 1),
-        compiler_params=pltpu.CompilerParams(vmem_limit_bytes=10 * MIB),
+        out_specs=[vmem] * plan.near,
+        out_shape=[jax.ShapeDtypeStruct(shape, dtype) for dtype in types],
+        compiler_params=pltpu.CompilerParams(vmem_limit_bytes=6 * MIB),
     )(keep, got)
 
 
@@ -388,16 +450,21 @@
         return lax.ppermute(value, axis, [(i, i ^ bit) for i in range(mesh.shape[axis])])
 
     metas = [meta] + [swap(meta, "visit", d) for d in range(1, plan.visits)]
-    sources = []
     chunks = [(lo, min(hi, count)) for lo, hi in CHUNKS]
-    for chunk in chunks:
-        slots = match(plan, chunk, row_offset, sides, factors, images, table, rows)
-        sources += [slots[0]] + [swap(slots[d], "visit", d) for d in range(1, plan.visits)]
+    ready, last = [], []
+    for n, (lo, hi) in enumerate(chunks):
+        slots = match(plan, (lo, hi), True, row_offset, sides, factors, images, table, rows)
+        ready.append(((0, lo, hi), slots[0]))
+        group = last if n == len(chunks) - 1 else ready
+        group += [((d, lo, hi), swap(slots[d], "visit", d)) for d in range(1, plan.visits)]
+    strip = early(plan, [job for job, _ in ready], count, metas, [source for _, source in ready])
+    send_far, send_near, keep_far, keep_near = late(plan, [job for job, _ in last], count, metas, [source for _, source in last], strip)
     cover = cover_of(plan, metas)
-    send, keep = place(plan, chunks, count, metas, sources)
-    folded = fold(plan, keep, swap(send, "patch", 1))
-    parts = [swap(folded[m], "patch", 2 * m) for m in range(1, plan.patches // 2)]
-    return finish(plan, cover, folded[0], parts)
+    far = fold(plan, keep_far, swap(send_far, "patch", 1), False)
+    near = fold(plan, keep_near, swap(send_near, "patch", 1), True)
+    folded = list(near) + list(far)
+    parts = [swap(folded[m], "patch", 2 * m) for m in range(2 * plan.near - 1, 0, -1)]
+    return finish(plan, cover, near[0], parts)
 
 
 def solution(mesh):

time: 53.9 us -> 54.9 us (1.019)
  Pallas kernels: 16.8 us -> 22.1 us
  waiting for transfers between devices: 13.6 us -> 9.53 us
  local copies, waits for them, and re-layouts: 5.43 us -> 2.02 us
  starting transfers between devices: 16.9 us -> 20.2 us
    ppermute x11 -> x12, waiting for transfers between devices: 13.6 us -> 9.53 us  [swap(): lax.ppermute(value, axis, [(i, i ^ bit) for i in range(mesh.shape[axis])])]
    unnamed x18 -> x14, local copies, waits for them, and re-layouts: 5.31 us -> 1.9 us
    ppermute x11 -> x12, starting transfers between devices: 16.9 us -> 20.2 us  [swap(): lax.ppermute(value, axis, [(i, i ^ bit) for i in range(mesh.shape[axis])])]
    pallas_call x2, Pallas kernels: 10.5 us -> 13.3 us  [match(): pl.pallas_call(functools.partial(match_kernel, plan, first, images.shape[...]
    pallas_call x1 -> x2, Pallas kernels: 3.81 us -> 6.25 us  [the longest x1 3.15 us: late(): pl.pallas_call(functools.partial(late_kernel, plan, jobs, total), name='l...]
  transfers between devices with their start and end apart: 11 -> 12, of which waited for: 4 -> 5; matrix products, arithmetic and copies ran while one was open for 0% -> 0% of each run, Pallas kernels for 12% -> 20%
where the time goes in v3:
time: 54.9 us; the launch traced here: 54.7 us
  Pallas kernels  22.1 us (40%)
  starting transfers between devices  20.2 us (37%)
  waiting for transfers between devices  9.53 us (17%)
  local copies, waits for them, and re-layouts  2.02 us (4%)
  between operations  0.82 us (1%)
    ppermute x12, starting transfers between devices, swap(): lax.ppermute(value, axis, [(i, i ^ bit) for i in range(mesh.shape[axis])])  20.2 us
    pallas_call x2, Pallas kernels, match(): pl.pallas_call(functools.partial(match_kernel, plan, first, images.shape[...  13.3 us
    ppermute x12, waiting for transfers between devices, swap(): lax.ppermute(value, axis, [(i, i ^ bit) for i in range(mesh.shape[axis])])  9.53 us
    pallas_call x1, Pallas kernels, late(): pl.pallas_call(functools.partial(late_kernel, plan, jobs, total), name='l...  3.15 us
    pallas_call x1, Pallas kernels, early(): pl.pallas_call(functools.partial(early_kernel, plan, jobs, total), name='...  3.11 us
    unnamed x14, local copies, waits for them, and re-layouts  1.9 us
    pallas_call x1, Pallas kernels, finish(): pl.pallas_call(functools.partial(finish_kernel, plan, filt), name='finish...  1.42 us
  transfers between devices with their start and end apart: 12, of which 5 were waited for; matrix products, arithmetic and copies ran while one was open for 0% of the time, Pallas kernels for 20%

profile of v3, /device:TPU:0, one launch (start us, length us, event | category | flops | bytes accessed | tf_op | source)
XLA Modules:
  0.0 54.7 jit_solution(15564947133659258043)
XLA Ops:
  0.6 0.0 copy-start.3
  0.6 0.0 copy-start.2
  0.7 0.0 copy-start.5
  0.7 0.0 copy-start.6
  0.7 0.0 copy-start.4
  0.7 6.7 %match.3 = (bf16[3,72,512]{2,1,0:T(8,128)(2,1)}, bf16[3,72,512]{2,1,0:T(8,128)(2,1)}) custom-call(s32[1,96]{1,0:T(1,128)} %refs_0_.3, f32[1,2,96]{2,1,0:T(2,128)} %bitcast.21, f32[6,3,1,40]{3,2,1,0:T(1,128)} %bitcast.19, bf16[1,6,128,512]{3,2,1,0:T(8,128)(2,1)} %refs_3_.3, bf16[256,2048]{1,0:T(8,128)(2,1)} %constant.10.clone.refs_4_, ...), custom_call_target="tpu_custom_call" | custom-call | tf_op jit(solution)/shard_map/match/pallas_call | solution.py:189
  7.4 3.0 %collective-permute-start.2 = (bf16[3,72,512]{2,1,0:T(8,128)(2,1)}, bf16[3,72,512]{2,1,0:T(8,128)(2,1)S(1)}, u32[]{:S(2)}, u32[]{:S(2)}) collective-permute-start(bf16[3,72,512]{2,1,0:T(8,128)(2,1)} %get-tuple-element.20), channel_id=1, source_target_pairs={{0,16},{16,0},{1,17},{17,1},{2,18},{18,2},{3,19},{19,3},{4,20},{20... | collective-permute-start | bytes 663560 | tf_op jit(solution)/shard_map/ppermute | solution.py:450
  10.4 6.6 %match.2 = (bf16[3,72,512]{2,1,0:T(8,128)(2,1)}, bf16[3,72,512]{2,1,0:T(8,128)(2,1)}) custom-call(s32[1,96]{1,0:T(1,128)} %refs_0_.3, f32[1,2,96]{2,1,0:T(2,128)} %bitcast.22, f32[6,3,1,40]{3,2,1,0:T(1,128)} %bitcast.20, bf16[1,6,128,512]{3,2,1,0:T(8,128)(2,1)} %refs_3_.3, bf16[256,2048]{1,0:T(8,128)(2,1)} %constant.10.clone.refs_4_, ...), custom_call_target="tpu_custom_call" | custom-call | tf_op jit(solution)/shard_map/match/pallas_call | solution.py:189
  17.0 0.1 collective-permute-start.1
  17.1 0.0 copy-done.2
  17.1 0.0 copy-done.5
  17.1 0.0 copy-done.6
  17.2 0.0 copy-done.3
  17.2 0.0 copy-done.4
  17.2 0.1 copy.21.refs_0_
  17.3 2.1 %collective-permute-start = (f32[96,8]{1,0:T(8,128)S(1)}, f32[96,8]{1,0:T(8,128)S(1)}, u32[]{:S(2)}, u32[]{:S(2)}) collective-permute-start(f32[96,8]{1,0:T(8,128)S(1)} %copy.21.refs_0_), channel_id=1, source_target_pairs={{0,16},{16,0},{1,17},{17,1},{2,18},{18,2},{3,19},{19,3},{4,20},{20... | collective-permute-start | bytes 9224 | tf_op jit(solution)/shard_map/ppermute | solution.py:450
  19.4 5.9 %collective-permute-done.refs_1_ = f32[96,8]{1,0:T(8,128)S(1)} collective-permute-done((f32[96,8]{1,0:T(8,128)S(1)}, f32[96,8]{1,0:T(8,128)S(1)}, u32[]{:S(2)}, u32[]{:S(2)}) %collective-permute-start) | collective-permute-done | bytes 3104 | tf_op jit(solution)/shard_map/ppermute | solution.py:450
  25.2 0.0 collective-permute-done.2.refs_3_
  25.2 0.0 copy-start
  25.2 0.9 %copy-done = bf16[3,72,512]{2,1,0:T(8,128)(2,1)S(1)} copy-done((bf16[3,72,512]{2,1,0:T(8,128)(2,1)S(1)}, bf16[3,72,512]{2,1,0:T(8,128)(2,1)}, u32[]{:S(2)}) %copy-start) | copy-done | bytes 221208
  26.2 0.0 copy-start.1
  26.2 0.9 %copy-done.1 = bf16[3,72,512]{2,1,0:T(8,128)(2,1)S(1)} copy-done((bf16[3,72,512]{2,1,0:T(8,128)(2,1)S(1)}, bf16[3,72,512]{2,1,0:T(8,128)(2,1)}, u32[]{:S(2)}) %copy-start.1) | copy-done | bytes 221208
  27.1 3.1 %early.1.refs_3_ = f32[66,72,128]{2,1,0:T(8,128)S(1)} custom-call(f32[96,8]{1,0:T(8,128)S(1)} %copy.21.refs_0_, f32[96,8]{1,0:T(8,128)S(1)} %collective-permute-done.refs_1_, bf16[3,72,512]{2,1,0:T(8,128)(2,1)S(1)} %copy-done, bf16[3,72,512]{2,1,0:T(8,128)(2,1)S(1)} %collective-permute-done.2.refs_3_, bf16[3,72,512]{2,1,0:T(8,128)(2,1)S(1)} %copy-done.1), custom_call_target="tpu_custom_call" | custom-call | tf_op jit(solution)/shard_map/early/pallas_call | solution.py:236
  30.2 0.0 collective-permute-done.1.refs_2_
  30.2 3.1 %late.1 = (f32[66,72,128]{2,1,0:T(8,128)S(1)}, bf16[4,72,512]{2,1,0:T(8,128)(2,1)S(1)}, bf16[4,72,512]{2,1,0:T(8,128)(2,1)S(1)}, f32[4,72,512]{2,1,0:T(8,128)S(1)}, f32[4,72,512]{2,1,0:T(8,128)S(1)}) custom-call(f32[96,8]{1,0:T(8,128)S(1)} %copy.21.refs_0_, f32[96,8]{1,0:T(8,128)S(1)} %collective-permute-done.refs_1_, ...), custom_call_target="tpu_custom_call", output_to_operand_aliasing={{0}: (3, {})} | custom-call | tf_op jit(solution)/shard_map/late/pallas_call | solution.py:291
  33.4 0.0 collective-permute-start.4
  33.4 0.5 collective-permute-start.3
  33.9 1.1 %collective-permute-done.4.got_ref = bf16[4,72,512]{2,1,0:T(8,128)(2,1)S(1)} collective-permute-done((bf16[4,72,512]{2,1,0:T(8,128)(2,1)S(1)}, bf16[4,72,512]{2,1,0:T(8,128)(2,1)S(1)}, u32[]{:S(2)}, u32[]{:S(2)}) %collective-permute-start.4) | collective-permute-done | bytes 294944 | tf_op jit(solution)/shard_map/ppermute | solution.py:450
  35.0 0.1 fold.3
  35.1 4.6 %collective-permute-start.5 = (bf16[72,512]{1,0:T(8,128)(2,1)S(1)}, bf16[72,512]{1,0:T(8,128)(2,1)S(1)}, u32[]{:S(2)}, u32[]{:S(2)}) collective-permute-start(bf16[72,512]{1,0:T(8,128)(2,1)S(1)} %get-tuple-element.27), channel_id=1, source_target_pairs={{0,14},{1,15},{2,12},{3,13},{4,10},{5,11},{6,8},{7,9},{8,6},{9,7},... | collective-permute-start | bytes 221192 | tf_op jit(solution)/shard_map/ppermute | solution.py:450
  39.7 0.2 collective-permute-start.6
  39.9 0.7 %collective-permute-start.7 = (bf16[72,512]{1,0:T(8,128)(2,1)S(1)}, bf16[72,512]{1,0:T(8,128)(2,1)S(1)}, u32[]{:S(2)}, u32[]{:S(2)}) collective-permute-start(bf16[72,512]{1,0:T(8,128)(2,1)S(1)} %get-tuple-element.29), channel_id=1, source_target_pairs={{0,10},{1,11},{2,8},{3,9},{4,14},{5,15},{6,12},{7,13},{8,2},{9,3},... | collective-permute-start | bytes 221192 | tf_op jit(solution)/shard_map/ppermute | solution.py:450
  40.6 2.1 %collective-permute-start.8 = (bf16[72,512]{1,0:T(8,128)(2,1)S(1)}, bf16[72,512]{1,0:T(8,128)(2,1)S(1)}, u32[]{:S(2)}, u32[]{:S(2)}) collective-permute-start(bf16[72,512]{1,0:T(8,128)(2,1)S(1)} %get-tuple-element.30), channel_id=1, source_target_pairs={{0,8},{1,9},{2,10},{3,11},{4,12},{5,13},{6,14},{7,15},{8,0},{9,1},... | collective-permute-start | bytes 221192 | tf_op jit(solution)/shard_map/ppermute | solution.py:450
  42.8 0.0 collective-permute-done.3.got_ref
  42.8 0.1 fold.2
  42.8 1.4 %collective-permute-start.10 = (bf16[72,512]{1,0:T(8,128)(2,1)S(1)}, bf16[72,512]{1,0:T(8,128)(2,1)S(1)}, u32[]{:S(2)}, u32[]{:S(2)}) collective-permute-start(bf16[72,512]{1,0:T(8,128)(2,1)S(1)} %get-tuple-element.32), channel_id=1, source_target_pairs={{0,4},{1,5},{2,6},{3,7},{4,0},{5,1},{6,2},{7,3},{8,12},{9,13},{10,... | collective-permute-start | bytes 221192 | tf_op jit(solution)/shard_map/ppermute | solution.py:450
  44.2 0.0 collective-permute-done.5.refs_0_
  44.2 1.5 %collective-permute-start.11 = (bf16[72,512]{1,0:T(8,128)(2,1)S(1)}, bf16[72,512]{1,0:T(8,128)(2,1)S(1)}, u32[]{:S(2)}, u32[]{:S(2)}) collective-permute-start(bf16[72,512]{1,0:T(8,128)(2,1)S(1)} %get-tuple-element.33), channel_id=1, source_target_pairs={{0,2},{1,3},{2,0},{3,1},{4,6},{5,7},{6,4},{7,5},{8,10},{9,11},{10,... | collective-permute-start | bytes 221192 | tf_op jit(solution)/shard_map/ppermute | solution.py:450
  45.7 0.8 %collective-permute-done.6.refs_1_ = bf16[72,512]{1,0:T(8,128)(2,1)S(1)} collective-permute-done((bf16[72,512]{1,0:T(8,128)(2,1)S(1)}, bf16[72,512]{1,0:T(8,128)(2,1)S(1)}, u32[]{:S(2)}, u32[]{:S(2)}) %collective-permute-start.6) | collective-permute-done | bytes 73760 | tf_op jit(solution)/shard_map/ppermute | solution.py:450
  46.5 4.0 %collective-permute-start.9 = (bf16[72,512]{1,0:T(8,128)(2,1)S(1)}, bf16[72,512]{1,0:T(8,128)(2,1)S(1)}, u32[]{:S(2)}, u32[]{:S(2)}) collective-permute-start(bf16[72,512]{1,0:T(8,128)(2,1)S(1)} %get-tuple-element.31), channel_id=1, source_target_pairs={{0,6},{1,7},{2,4},{3,5},{4,2},{5,3},{6,0},{7,1},{8,14},{9,15},{10,... | collective-permute-start | bytes 221192 | tf_op jit(solution)/shard_map/ppermute | solution.py:450
  50.5 1.0 %cover.1.cover_ref = f32[72,512]{1,0:T(8,128)S(1)} custom-call(f32[96,8]{1,0:T(8,128)S(1)} %copy.21.refs_0_, f32[96,8]{1,0:T(8,128)S(1)} %collective-permute-done.refs_1_), custom_call_target="tpu_custom_call" | custom-call | tf_op jit(solution)/shard_map/cover/pallas_call | solution.py:358
  51.5 0.0 collective-permute-done.7.refs_2_
  51.5 1.0 %collective-permute-done.8.refs_3_ = bf16[72,512]{1,0:T(8,128)(2,1)S(1)} collective-permute-done((bf16[72,512]{1,0:T(8,128)(2,1)S(1)}, bf16[72,512]{1,0:T(8,128)(2,1)S(1)}, u32[]{:S(2)}, u32[]{:S(2)}) %collective-permute-start.8) | collective-permute-done | bytes 73760 | tf_op jit(solution)/shard_map/ppermute | solution.py:450
  52.5 0.0 collective-permute-done.10.refs_5_
  52.5 0.0 collective-permute-done.11.refs_6_
  52.5 0.7 %collective-permute-done.9.refs_4_ = bf16[72,512]{1,0:T(8,128)(2,1)S(1)} collective-permute-done((bf16[72,512]{1,0:T(8,128)(2,1)S(1)}, bf16[72,512]{1,0:T(8,128)(2,1)S(1)}, u32[]{:S(2)}, u32[]{:S(2)}) %collective-permute-start.9) | collective-permute-done | bytes 73760 | tf_op jit(solution)/shard_map/ppermute | solution.py:450
  53.2 1.4 %finish.1 = (f32[64,512]{1,0:T(8,128)}, f32[64,512]{1,0:T(8,128)}) custom-call(f32[72,512]{1,0:T(8,128)S(1)} %cover.1.cover_ref, f32[72,512]{1,0:T(8,128)S(1)} %get-tuple-element.24.own_ref, bf16[72,512]{1,0:T(8,128)(2,1)S(1)} %collective-permute-done.5.refs_0_, bf16[72,512]{1,0:T(8,128)(2,1)S(1)} %collective-permute-done.6.refs_1_, ...), custom_call_target="tpu_custom_call" | custom-call | tf_op jit(solution)/shard_map/finish/pallas_call | solution.py:412
  (5 shorter events, 0.0 us)
Async XLA Ops:
  0.6 16.5 %copy-start.3 = (s32[1,96]{1,0:T(1,128)S(1)}, s32[1,96]{1,0:T(1,128)}, u32[]{:S(2)}) copy-start(s32[1,96]{1,0:T(1,128)} %refs_0_.3) | copy-start | bytes 1156
  0.6 16.5 %copy-start.2 = (f32[1,96,2]{1,2,0:T(2,128)S(1)}, f32[1,96,2]{1,2,0:T(2,128)}, u32[]{:S(2)}) copy-start(f32[1,96,2]{1,2,0:T(2,128)} %param.14) | copy-start | bytes 2308
  0.7 16.5 %copy-start.5 = (s32[1,96,2]{1,2,0:T(2,128)S(1)}, s32[1,96,2]{1,2,0:T(2,128)}, u32[]{:S(2)}) copy-start(s32[1,96,2]{1,2,0:T(2,128)} %param.11) | copy-start | bytes 2308
  0.7 16.5 %copy-start.6 = (s32[1,96]{1,0:T(1,128)S(1)}, s32[1,96]{1,0:T(1,128)}, u32[]{:S(2)}) copy-start(s32[1,96]{1,0:T(1,128)} %param.13) | copy-start | bytes 1156
  0.7 16.5 %copy-start.4 = (f32[1,96]{1,0:T(1,128)S(1)}, f32[1,96]{1,0:T(1,128)}, u32[]{:S(2)}) copy-start(f32[1,96]{1,0:T(1,128)} %param.15) | copy-start | bytes 1156
  7.4 17.9 %collective-permute-start.2 = (bf16[3,72,512]{2,1,0:T(8,128)(2,1)}, bf16[3,72,512]{2,1,0:T(8,128)(2,1)S(1)}, u32[]{:S(2)}, u32[]{:S(2)}) collective-permute-start(bf16[3,72,512]{2,1,0:T(8,128)(2,1)} %get-tuple-element.20), channel_id=1, source_target_pairs={{0,16},{16,0},{1,17},{17,1},{2,18},{18,2},{3,19},{19,3},{4,20},{20... | collective-permute-start | bytes 663560 | tf_op jit(solution)/shard_map/ppermute | solution.py:450
  17.0 13.2 %collective-permute-start.1 = (bf16[3,72,512]{2,1,0:T(8,128)(2,1)}, bf16[3,72,512]{2,1,0:T(8,128)(2,1)S(1)}, u32[]{:S(2)}, u32[]{:S(2)}) collective-permute-start(bf16[3,72,512]{2,1,0:T(8,128)(2,1)} %get-tuple-element.18), channel_id=1, source_target_pairs={{0,16},{16,0},{1,17},{17,1},{2,18},{18,2},{3,19},{19,3},{4,20},{20... | collective-permute-start | bytes 663560 | tf_op jit(solution)/shard_map/ppermute | solution.py:450
  17.3 7.9 %collective-permute-start = (f32[96,8]{1,0:T(8,128)S(1)}, f32[96,8]{1,0:T(8,128)S(1)}, u32[]{:S(2)}, u32[]{:S(2)}) collective-permute-start(f32[96,8]{1,0:T(8,128)S(1)} %copy.21.refs_0_), channel_id=1, source_target_pairs={{0,16},{16,0},{1,17},{17,1},{2,18},{18,2},{3,19},{19,3},{4,20},{20... | collective-permute-start | bytes 9224 | tf_op jit(solution)/shard_map/ppermute | solution.py:450
  25.2 0.9 %copy-start = (bf16[3,72,512]{2,1,0:T(8,128)(2,1)S(1)}, bf16[3,72,512]{2,1,0:T(8,128)(2,1)}, u32[]{:S(2)}) copy-start(bf16[3,72,512]{2,1,0:T(8,128)(2,1)} %get-tuple-element.19.refs_2_) | copy-start | bytes 663556
  26.2 0.9 %copy-start.1 = (bf16[3,72,512]{2,1,0:T(8,128)(2,1)S(1)}, bf16[3,72,512]{2,1,0:T(8,128)(2,1)}, u32[]{:S(2)}) copy-start(bf16[3,72,512]{2,1,0:T(8,128)(2,1)} %get-tuple-element.21.refs_4_) | copy-start | bytes 663556
  33.4 1.6 %collective-permute-start.4 = (bf16[4,72,512]{2,1,0:T(8,128)(2,1)S(1)}, bf16[4,72,512]{2,1,0:T(8,128)(2,1)S(1)}, u32[]{:S(2)}, u32[]{:S(2)}) collective-permute-start(bf16[4,72,512]{2,1,0:T(8,128)(2,1)S(1)} %get-tuple-element.26), channel_id=1, source_target_pairs={{0,1},{1,0},{2,3},{3,2},{4,5},{5,4},{6,7},{7,6},{8,9},{9,8},{10,11... | collective-permute-start | bytes 884744 | tf_op jit(solution)/shard_map/ppermute | solution.py:450
  33.4 9.3 %collective-permute-start.3 = (bf16[4,72,512]{2,1,0:T(8,128)(2,1)S(1)}, bf16[4,72,512]{2,1,0:T(8,128)(2,1)S(1)}, u32[]{:S(2)}, u32[]{:S(2)}) collective-permute-start(bf16[4,72,512]{2,1,0:T(8,128)(2,1)S(1)} %get-tuple-element.23), channel_id=1, source_target_pairs={{0,1},{1,0},{2,3},{3,2},{4,5},{5,4},{6,7},{7,6},{8,9},{9,8},{10,11... | collective-permute-start | bytes 884744 | tf_op jit(solution)/shard_map/ppermute | solution.py:450
  35.1 9.1 %collective-permute-start.5 = (bf16[72,512]{1,0:T(8,128)(2,1)S(1)}, bf16[72,512]{1,0:T(8,128)(2,1)S(1)}, u32[]{:S(2)}, u32[]{:S(2)}) collective-permute-start(bf16[72,512]{1,0:T(8,128)(2,1)S(1)} %get-tuple-element.27), channel_id=1, source_target_pairs={{0,14},{1,15},{2,12},{3,13},{4,10},{5,11},{6,8},{7,9},{8,6},{9,7},... | collective-permute-start | bytes 221192 | tf_op jit(solution)/shard_map/ppermute | solution.py:450
  39.7 6.8 %collective-permute-start.6 = (bf16[72,512]{1,0:T(8,128)(2,1)S(1)}, bf16[72,512]{1,0:T(8,128)(2,1)S(1)}, u32[]{:S(2)}, u32[]{:S(2)}) collective-permute-start(bf16[72,512]{1,0:T(8,128)(2,1)S(1)} %get-tuple-element.28), channel_id=1, source_target_pairs={{0,12},{1,13},{2,14},{3,15},{4,8},{5,9},{6,10},{7,11},{8,4},{9,5},... | collective-permute-start | bytes 221192 | tf_op jit(solution)/shard_map/ppermute | solution.py:450
  39.9 11.6 %collective-permute-start.7 = (bf16[72,512]{1,0:T(8,128)(2,1)S(1)}, bf16[72,512]{1,0:T(8,128)(2,1)S(1)}, u32[]{:S(2)}, u32[]{:S(2)}) collective-permute-start(bf16[72,512]{1,0:T(8,128)(2,1)S(1)} %get-tuple-element.29), channel_id=1, source_target_pairs={{0,10},{1,11},{2,8},{3,9},{4,14},{5,15},{6,12},{7,13},{8,2},{9,3},... | collective-permute-start | bytes 221192 | tf_op jit(solution)/shard_map/ppermute | solution.py:450
  40.6 11.9 %collective-permute-start.8 = (bf16[72,512]{1,0:T(8,128)(2,1)S(1)}, bf16[72,512]{1,0:T(8,128)(2,1)S(1)}, u32[]{:S(2)}, u32[]{:S(2)}) collective-permute-start(bf16[72,512]{1,0:T(8,128)(2,1)S(1)} %get-tuple-element.30), channel_id=1, source_target_pairs={{0,8},{1,9},{2,10},{3,11},{4,12},{5,13},{6,14},{7,15},{8,0},{9,1},... | collective-permute-start | bytes 221192 | tf_op jit(solution)/shard_map/ppermute | solution.py:450
  42.8 9.7 %collective-permute-start.10 = (bf16[72,512]{1,0:T(8,128)(2,1)S(1)}, bf16[72,512]{1,0:T(8,128)(2,1)S(1)}, u32[]{:S(2)}, u32[]{:S(2)}) collective-permute-start(bf16[72,512]{1,0:T(8,128)(2,1)S(1)} %get-tuple-element.32), channel_id=1, source_target_pairs={{0,4},{1,5},{2,6},{3,7},{4,0},{5,1},{6,2},{7,3},{8,12},{9,13},{10,... | collective-permute-start | bytes 221192 | tf_op jit(solution)/shard_map/ppermute | solution.py:450
  44.2 8.3 %collective-permute-start.11 = (bf16[72,512]{1,0:T(8,128)(2,1)S(1)}, bf16[72,512]{1,0:T(8,128)(2,1)S(1)}, u32[]{:S(2)}, u32[]{:S(2)}) collective-permute-start(bf16[72,512]{1,0:T(8,128)(2,1)S(1)} %get-tuple-element.33), channel_id=1, source_target_pairs={{0,2},{1,3},{2,0},{3,1},{4,6},{5,7},{6,4},{7,5},{8,10},{9,11},{10,... | collective-permute-start | bytes 221192 | tf_op jit(solution)/shard_map/ppermute | solution.py:450
  46.5 6.7 %collective-permute-start.9 = (bf16[72,512]{1,0:T(8,128)(2,1)S(1)}, bf16[72,512]{1,0:T(8,128)(2,1)S(1)}, u32[]{:S(2)}, u32[]{:S(2)}) collective-permute-start(bf16[72,512]{1,0:T(8,128)(2,1)S(1)} %get-tuple-element.31), channel_id=1, source_target_pairs={{0,6},{1,7},{2,4},{3,5},{4,2},{5,3},{6,0},{7,1},{8,14},{9,15},{10,... | collective-permute-start | bytes 221192 | tf_op jit(solution)/shard_map/ppermute | solution.py:450
